TPU v7x, 32 devices: a whole 2x2x4 slice. The times are simulated.
32 devices in a mesh: ex: 8 (over z, y), tp: 4 (over x, core).
Axes of the slice: x: 2, y: 2, z: 4, core: 2. Of those that a mesh axis runs over, the one named last changes fastest.
Arguments:
- residual_in: bfloat16 [1536, 2880], P('ex', 'tp'), may hold values from -40 to 40
- queries: bfloat16 [1536, 2048], P('ex', 'tp'), may hold values from -4 to 4
- keys_values: bfloat16 [1536, 4, 128], P('ex', 'tp'), may hold values from -4 to 4
- sink_logits: float32 [32], P('tp'), may hold values from 1 to 6
- out_proj: bfloat16 [2048, 2880], P('tp'), may hold values from -0.75 to 0.75
- norm_gain: float32 [2880], replicated, may hold values from 0.25 to 1.75
- routes: int32 [1536, 4], P('ex'), may hold values from 0 to 7, all different within a row; in each aligned block of 192 rows (0 to 191, 192 to 383, ...) at most 160 rows name the same one
- route_scores: int32 [1536, 4], P('ex'), may hold values from 1 to 8
- tenants: int32 [1536], P('ex'), may hold values from 0 to 7
- gate_up: bfloat16 [8, 2880, 2, 1536], P('ex', None, None, 'tp'), may hold values from -0.109375 to 0.109375
- adapter_in: bfloat16 [8, 2880, 128], P('ex'), may hold values from -0.109375 to 0.109375
- adapter_out: bfloat16 [8, 128, 2, 1536], P('ex', None, None, 'tp'), may hold values from -1.5 to 1.5
- down_proj: bfloat16 [8, 1536, 2880], P('ex', 'tp'), may hold values from -0.15625 to 0.15625
Outputs:
- residual_out: bfloat16 [1536, 2880], P('ex', 'tp')
- expert_mix: bfloat16 [1536, 2880], P('ex', 'tp')
Inputs may be any that keep to these rules, and one draw needn't show every extreme that they name: `routes`: among the 192 rows of one device (aligned blocks), no expert is named by more than 160 rows, and in every draw some expert is named by exactly 160 rows of some block.
All inputs are finite; a program needn't handle non-finite values.
Results may differ from a plain program's by a relative error of at most 0.023.
Values may be sent and summed in bfloat16 or wider, within the bound.
A program may use at most 128 MiB of HBM per device.

v0:
```python
import jax
import jax.numpy as jnp
from jax import lax
from jax.sharding import PartitionSpec as P

WINDOW = 128
TOP = 4
RANK = 16


def from_behind(value, axis, steps):
    count = lax.axis_size(axis)
    initial, last = (max(0, -steps), min(count, count - steps))
    return lax.ppermute(value, axis, [(source, source + steps) for source in range(initial, last)])


def shards(
    residual_in,
    queries,
    keys_values,
    sink_logits,
    out_proj,
    norm_gain,
    routes,
    route_scores,
    tenants,
    gate_up,
    adapter_in,
    adapter_out,
    down_proj,
):
    tok_rows = residual_in.shape[0]
    columns = residual_in.shape[1]
    width = out_proj.shape[1]
    heads_here = sink_logits.shape[0]
    kv_here = keys_values.shape[1]
    group_size = heads_here // kv_here
    head_size = keys_values.shape[2] // 2
    rim_rows = WINDOW - 1
    before = from_behind(keys_values[tok_rows - rim_rows :], "ex", 1)
    extended = jnp.concatenate([before, keys_values], axis=0)
    keys_only = extended[:, :, :head_size]
    values_only = extended[:, :, head_size:]
    query_rows = queries.reshape(tok_rows, kv_here, group_size, head_size)
    scores = jnp.einsum(
        "tcgd,jcd->cgtj", query_rows, keys_only, preferred_element_type=jnp.float32
    ) * head_size ** (-0.5)
    start = lax.axis_index("ex") * tok_rows
    query_pos = start + jnp.arange(tok_rows, dtype=jnp.int32)
    key_pos = start - rim_rows + jnp.arange(tok_rows + rim_rows, dtype=jnp.int32)
    distance = query_pos[:, None] - key_pos[None, :]
    allowed = (distance >= 0) & (distance < WINDOW) & (key_pos[None, :] >= 0)
    numerators = jnp.where(allowed, jnp.exp(scores), 0.0)
    totals = jnp.exp(sink_logits.reshape(kv_here, group_size))[:, :, None] + jnp.sum(
        numerators, axis=-1
    )
    weights = (numerators / totals[..., None]).astype(jnp.bfloat16)
    attended = jnp.einsum(
        "cgtj,jcd->tcgd", weights, values_only, preferred_element_type=jnp.float32
    )
    attended = attended.astype(jnp.bfloat16).reshape(tok_rows, heads_here * head_size)
    head_terms = jnp.dot(attended, out_proj, preferred_element_type=jnp.float32)
    head_share = lax.psum_scatter(
        head_terms.astype(jnp.bfloat16), "tp", scatter_dimension=1, tiled=True
    ).astype(jnp.float32)
    residual_out = (residual_in.astype(jnp.float32) + head_share).astype(jnp.bfloat16)
    whole_rows = lax.all_gather(residual_out, "tp", axis=1, tiled=True).astype(jnp.float32)
    inverse = lax.rsqrt(jnp.mean(whole_rows * whole_rows, axis=-1, keepdims=True) + 1e-05)
    normed = (whole_rows * inverse * norm_gain).astype(jnp.bfloat16)
    sources = lax.axis_size("ex")
    local_count = gate_up.shape[0]
    experts_all = local_count * sources
    capacity = 5 * tok_rows * TOP // (3 * experts_all)
    pair_count = tok_rows * TOP
    route_flat = routes.reshape(pair_count)
    one_hot = (route_flat[:, None] == jnp.arange(experts_all, dtype=jnp.int32)[None, :]).astype(
        jnp.int32
    )
    earlier = jnp.cumsum(one_hot, axis=0) - one_hot
    slot = jnp.sum(earlier * one_hot, axis=1)
    target = route_flat * capacity + slot
    pair_of = (
        jnp.full((experts_all * capacity,), pair_count, jnp.int32)
        .at[target]
        .set(jnp.arange(pair_count, dtype=jnp.int32))
    )
    token_of = pair_of // TOP
    send_width = normed.shape[1]
    normed_pad = jnp.concatenate([normed, jnp.zeros((1, send_width), jnp.bfloat16)], axis=0)
    tenant_pad = jnp.concatenate([tenants, jnp.zeros((1,), jnp.int32)])
    sent_rows = normed_pad[token_of].reshape(experts_all, capacity, send_width)
    sent_tenants = tenant_pad[token_of].reshape(experts_all, capacity)
    received, got_tenants = (
        lax.all_to_all(sent_rows, "ex", split_axis=0, concat_axis=0, tiled=True),
        lax.all_to_all(sent_tenants, "ex", split_axis=0, concat_axis=0, tiled=True),
    )
    hidden_here = gate_up.shape[3]
    rank_cols = adapter_in.shape[2]
    arrived = received.reshape(sources, local_count, capacity, width)
    arrived_tenants = got_tenants.reshape(sources, local_count, capacity)
    slot_rows = arrived[:, 0].reshape(sources * capacity, width)
    slot_tenant = arrived_tenants[:, 0].reshape(sources * capacity)
    mapped = jnp.dot(
        slot_rows, gate_up[0].reshape(width, 2 * hidden_here), preferred_element_type=jnp.float32
    )
    low_rank = jnp.dot(slot_rows, adapter_in[0], preferred_element_type=jnp.float32)
    keep = (jnp.arange(rank_cols, dtype=jnp.int32) // RANK)[None, :] == slot_tenant[:, None]
    low_rank = jnp.where(keep, low_rank, 0.0).astype(jnp.bfloat16)
    mapped = mapped + jnp.dot(
        low_rank,
        adapter_out[0].reshape(rank_cols, 2 * hidden_here),
        preferred_element_type=jnp.float32,
    )
    gate_part = mapped[:, :hidden_here]
    up_part = mapped[:, hidden_here:]
    activated = (gate_part * jax.nn.sigmoid(1.702 * gate_part) * (up_part + 1.0)).astype(
        jnp.bfloat16
    )
    quarter = jnp.dot(activated, down_proj[0], preferred_element_type=jnp.float32).astype(
        jnp.bfloat16
    )
    outputs = quarter.reshape(sources, 1, capacity, width)
    quarters = outputs.reshape(sources * local_count, capacity, width)
    score_float = route_scores.astype(jnp.float32)
    route_weight = (score_float / jnp.sum(score_float, axis=1, keepdims=True)).reshape(pair_count)
    shares = lax.psum_scatter(
        quarters.astype(jnp.float32).astype(jnp.bfloat16), "tp", scatter_dimension=2, tiled=True
    ).astype(jnp.float32)
    returned = lax.all_to_all(
        shares.astype(jnp.bfloat16), "ex", split_axis=0, concat_axis=0, tiled=True
    ).astype(shares.dtype)
    picked = returned.reshape(experts_all * capacity, columns)[target]
    expert_mix = jnp.sum((picked * route_weight[:, None]).reshape(tok_rows, TOP, columns), axis=1)
    return (residual_out, expert_mix.astype(jnp.bfloat16))


def solution(mesh):
    in_specs = (
        P("ex", "tp"),
        P("ex", "tp"),
        P("ex", "tp", None),
        P("tp"),
        P("tp", None),
        P(),
        P("ex", None),
        P("ex", None),
        P("ex"),
        P("ex", None, None, "tp"),
        P("ex", None, None),
        P("ex", None, None, "tp"),
        P("ex", "tp", None),
    )
    out_specs = (P("ex", "tp"), P("ex", "tp"))
    return jax.shard_map(shards, mesh=mesh, in_specs=in_specs, out_specs=out_specs, check_vma=False)
```

profile of v0, /device:TPU:0, one launch (start us, length us, event | category | flops | bytes accessed | tf_op | source)
XLA Modules:
  0.0 482.4 jit_solution(15424378577846066376)
XLA Ops:
  7.2 1.0 copy.33
  8.4 4.9 %collective-permute-start = (bf16[127,1,128]{0,2,1:T(8,128)(2,1)S(1)}, bf16[127,1,128]{0,2,1:T(8,128)(2,1)S(1)}, u32[]{:S(2)}, u32[]{:S(2)}) collective-permute-start(bf16[127,1,128]{0,2,1:T(8,128)(2,1)S(1)} %slice.34), channel_id=1, source_target_pairs={{0,4},{4,8},{8,12},{12,16},{16,20},{20,24},{24,28},{1,5},{5,9},{9,... | collective-permute-start | bytes 97544 | tf_op jit(solution)/shard_map/ppermute | solution.py:14
  13.3 0.1 fusion.17
  13.5 1.1 copy.35
  14.5 0.7 exp.19
  15.2 0.9 fusion.4
  16.2 0.8 convolution_convert_fusion.2
  17.0 2.1 convolution_convert_fusion.1
  19.1 2.5 copy.44
  21.8 29.2 %reduce-scatter.7.cloned.1.call-done = bf16[720,192]{1,0:T(8,128)(2,1)} async-done(((bf16[2880,192]{1,0:T(8,128)(2,1)}), bf16[720,192]{1,0:T(8,128)(2,1)}) %reduce-scatter.7.cloned.1.call-update) | async-done | bytes 276496
  51.0 1.1 copy.45
  52.1 0.8 add_convert_fusion
  52.9 0.1 copy.38
  53.1 0.1 eq.44
  53.2 0.1 eq.40
  53.3 1.7 reduce-window.6
  55.1 0.1 copy.40
  55.2 0.2 reduce-window.9
  55.5 0.1 copy.37
  55.6 0.1 mul.80
  55.9 3.4 scatter_custom_fusion
  59.4 7.9 %gather_fusion.1 = s32[1280]{0:T(1024)S(1)} fusion(s32[193]{0:T(256)S(1)} %pad_add_fusion, s32[2048]{0:T(1024)S(1)} %pad_clamp_fusion), kind=kCustom, calls=%fused_computation.1 | custom fusion | bytes 15360 | tf_op jit(solution)/shard_map/gather | solution.py:92
  67.3 0.7 all_to_all.13
  68.0 5.5 %all-to-all-start.1 = ((s32[8,1,160]{2,1,0:T(1,128)}), s32[8,1,160]{2,1,0:T(1,128)S(1)}, u32[]{:S(2)}, u32[]{:S(2)}) async-start(s32[8,1,160]{2,1,0:T(1,128)} %all_to_all.13), calls=%async_computation.1 | async-start | bytes 16384 | tf_op jit(solution)/shard_map/all_to_all | solution.py:95
  73.5 3.6 copy.36
  77.1 3.0 reshape.206
  80.1 0.2 multiply_reduce_fusion.1
  80.4 0.3 fusion.6
  80.8 7.1 %gather_fusion = bf16[1280,2880]{1,0:T(8,128)(2,1)} fusion(bf16[193,2880]{1,0:T(8,128)(2,1)S(1)} %concatenate.10, s32[2048]{0:T(1024)S(1)} %pad_clamp_fusion), kind=kCustom, calls=%fused_computation | custom fusion | bytes 14750720 | tf_op jit(solution)/shard_map/gather | solution.py:91
  87.8 6.0 %all-to-all-start = ((bf16[8,160,2880]{2,1,0:T(8,128)(2,1)}), bf16[8,160,2880]{2,1,0:T(8,128)(2,1)}, u32[]{:S(2)}, u32[]{:S(2)}) async-start(bf16[8,160,2880]{2,1,0:T(8,128)(2,1)} %bitcast.78), calls=%async_computation | async-start | bytes 15073280 | tf_op jit(solution)/shard_map/all_to_all | solution.py:94
  93.8 5.1 %copy.48 = bf16[360,8,2,384]{3,1,2,0:T(8,128)(2,1)} copy(bf16[360,8,2,384]{3,2,1,0:T(2,128)(2,1)} %bitcast.82) | data formatting | bytes 8847360
  99.1 158.9 %all-to-all-done = bf16[8,160,2880]{2,1,0:T(8,128)(2,1)} async-done(((bf16[8,160,2880]{2,1,0:T(8,128)(2,1)}), bf16[8,160,2880]{2,1,0:T(8,128)(2,1)}, u32[]{:S(2)}, u32[]{:S(2)}) %all-to-all-start) | async-done | bytes 7372832 | tf_op jit(solution)/shard_map/all_to_all | solution.py:94
  258.0 11.2 %fusion.40 = f32[1280,768]{1,0:T(8,128)} fusion(bf16[1280,2880]{1,0:T(8,128)(2,1)} %bitcast.18, bf16[2880,768]{1,0:T(8,128)(2,1)} %bitcast.83), kind=kOutput, calls=%fused_computation.83 | convolution fusion | flops 5662310400 | bytes 15728640 | tf_op jit(solution)/shard_map/dot_general | solution.py:103
  269.2 9.7 %convolution_add_fusion = f32[1280,768]{1,0:T(8,128)} fusion(f32[1280,768]{1,0:T(8,128)} %fusion.40, bf16[128,768]{1,0:T(8,128)(2,1)S(1)} %bitcast.85, bf16[1280,2880]{1,0:T(8,128)(2,1)} %bitcast.18, bf16[1,2880,128]{2,1,0:T(8,128)(2,1)S(1)} %copy-done.2, s32[128]{0:T(128)S(1)} %and_select_fusion, s32[1280]{0:T(1024)S(1)} %eq.49), kind=kOutput, calls=%fused_computation.5 | convolution fusion | flops 1196851200 | bytes 16176640 | tf_op jit(solution)/shard_map/dot_general | solution.py:109
  278.9 9.9 %convolution_convert_fusion = bf16[1280,2880]{0,1:T(8,128)(2,1)} fusion(bf16[1,384,2880]{1,2,0:T(8,128)(2,1)} %param.25, f32[1280,768]{1,0:T(8,128)} %convolution_add_fusion), kind=kOutput, calls=%fused_computation.4 | convolution fusion | flops 2838773760 | bytes 13516800 | tf_op jit(solution)/shard_map/dot_general | solution.py:119
  288.7 10.4 %copy.42 = bf16[1280,2880]{1,0:T(8,128)(2,1)} copy(bf16[1280,2880]{0,1:T(8,128)(2,1)} %convolution_convert_fusion) | data formatting | bytes 14745600 | tf_op jit(solution)/shard_map/convert_element_type | solution.py:119
  299.2 17.1 %copy.46 = bf16[8,160,2880]{1,0,2:T(8,128)(2,1)} copy(bf16[8,160,2880]{2,1,0:T(8,128)(2,1)} %bitcast.79) | data formatting | bytes 14745600
  316.3 19.1 %reshape.211 = bf16[2880,1280]{1,0:T(8,128)(2,1)} reshape(bf16[2880,8,160]{2,1,0:T(8,128)(2,1)} %bitcast.77) | data formatting | bytes 14745600
  335.4 64.4 %reduce-scatter.9.cloned.1.call-done = bf16[720,1280]{1,0:T(8,128)(2,1)} async-done(((bf16[2880,1280]{1,0:T(8,128)(2,1)}), bf16[720,1280]{1,0:T(8,128)(2,1)}) %reduce-scatter.9.cloned.1.call-update) | async-done | bytes 1843216
  399.9 5.1 %reshape.212 = bf16[720,8,160]{2,1,0:T(8,128)(2,1)S(1)} reshape(bf16[720,1280]{1,0:T(8,128)(2,1)} %reduce-scatter.9.cloned.1.call-done) | data formatting | bytes 3686400
  405.0 3.8 copy.47
  408.7 5.6 %all-to-all-start.2 = ((bf16[8,160,720]{2,1,0:T(8,128)(2,1)}), bf16[8,160,720]{2,1,0:T(8,128)(2,1)S(1)}, u32[]{:S(2)}, u32[]{:S(2)}) async-start(bf16[8,160,720]{2,1,0:T(8,128)(2,1)} %copy.47), calls=%async_computation.2 | async-start | bytes 3932160 | tf_op jit(solution)/shard_map/all_to_all | solution.py:129
  414.4 0.1 copy.43
  414.6 45.1 %all-to-all-done.2 = bf16[8,160,720]{2,1,0:T(8,128)(2,1)S(1)} async-done(((bf16[8,160,720]{2,1,0:T(8,128)(2,1)}), bf16[8,160,720]{2,1,0:T(8,128)(2,1)S(1)}, u32[]{:S(2)}, u32[]{:S(2)}) %all-to-all-start.2) | async-done | bytes 1843232 | tf_op jit(solution)/shard_map/all_to_all | solution.py:129
  459.7 2.3 bitcast_convert_fusion
  462.0 6.2 %gather_fusion.2 = f32[768,720]{1,0:T(8,128)} fusion(f32[1280,720]{1,0:T(8,128)} %bitcast_convert_fusion, s32[1024]{0:T(1024)S(1)} %pad_clamp_fusion.1), kind=kCustom, calls=%fused_computation.2 | custom fusion | bytes 4426752 | tf_op jit(solution)/shard_map/gather | solution.py:132
  468.2 3.8 gather.14
  472.0 3.9 multiply_reduce_fusion
  (51 shorter events, 1.0 us)
Async XLA Ops:
  7.2 9.9 %copy-start = (bf16[512,2880]{0,1:T(8,128)(2,1)S(1)}, bf16[512,2880]{0,1:T(8,128)(2,1)}, u32[]{:S(2)}) copy-start(bf16[512,2880]{0,1:T(8,128)(2,1)} %param.17) | copy-start | bytes 8847364
  7.2 43.8 %reduce-scatter.7.cloned.1.call-start = ((), (), s32[]{:S(2)}) async-start(), calls=%async_computation.6 | async-start | bytes 1843200
  8.4 6.8 %collective-permute-start = (bf16[127,1,128]{0,2,1:T(8,128)(2,1)S(1)}, bf16[127,1,128]{0,2,1:T(8,128)(2,1)S(1)}, u32[]{:S(2)}, u32[]{:S(2)}) collective-permute-start(bf16[127,1,128]{0,2,1:T(8,128)(2,1)S(1)} %slice.34), channel_id=1, source_target_pairs={{0,4},{4,8},{8,12},{12,16},{16,20},{20,24},{24,28},{1,5},{5,9},{9,... | collective-permute-start | bytes 97544 | tf_op jit(solution)/shard_map/ppermute | solution.py:14
  19.1 33.0 %copy-start.3 = (bf16[192,720]{1,0:T(8,128)(2,1)S(1)}, bf16[192,720]{1,0:T(8,128)(2,1)}, u32[]{:S(2)}) copy-start(bf16[192,720]{1,0:T(8,128)(2,1)} %param.13) | copy-start | bytes 829444
  19.1 33.8 %copy-start.5 = (s32[192,4]{0,1:T(4,128)S(1)}, s32[192,4]{0,1:T(4,128)}, u32[]{:S(2)}) copy-start(s32[192,4]{0,1:T(4,128)} %param.19) | copy-start | bytes 9220
  21.7 37.6 %copy-start.8 = (s32[192]{0:T(256)S(1)}, s32[192]{0:T(256)}, u32[]{:S(2)}) copy-start(s32[192]{0:T(256)} %param.21) | copy-start | bytes 2308
  21.7 51.8 %all-gather.3.cloned.1.call-start = ((), (), s32[]{:S(2)}) async-start(), calls=%async_computation.5 | async-start | bytes 1474560 | tf_op jit(solution)/shard_map/all_gather | solution.py:67
  68.0 19.8 %all-to-all-start.1 = ((s32[8,1,160]{2,1,0:T(1,128)}), s32[8,1,160]{2,1,0:T(1,128)S(1)}, u32[]{:S(2)}, u32[]{:S(2)}) async-start(s32[8,1,160]{2,1,0:T(1,128)} %all_to_all.13), calls=%async_computation.1 | async-start | bytes 16384 | tf_op jit(solution)/shard_map/all_to_all | solution.py:95
  77.1 3.3 copy-start.7
  87.8 170.2 %all-to-all-start = ((bf16[8,160,2880]{2,1,0:T(8,128)(2,1)}), bf16[8,160,2880]{2,1,0:T(8,128)(2,1)}, u32[]{:S(2)}, u32[]{:S(2)}) async-start(bf16[8,160,2880]{2,1,0:T(8,128)(2,1)} %bitcast.78), calls=%async_computation | async-start | bytes 15073280 | tf_op jit(solution)/shard_map/all_to_all | solution.py:94
  93.8 306.1 %reduce-scatter.9.cloned.1.call-start = ((), (), s32[]{:S(2)}) async-start(), calls=%async_computation.7 | async-start | bytes 9216000
  93.8 5.1 %copy-start.4 = (bf16[1,128,2,384]{3,2,1,0:T(2,128)(2,1)S(1)}, bf16[1,128,2,384]{3,2,1,0:T(2,128)(2,1)}, u32[]{:S(2)}) copy-start(bf16[1,128,2,384]{3,2,1,0:T(2,128)(2,1)} %param.24) | copy-start | bytes 589828
  258.0 11.2 %copy-start.2 = (bf16[1,2880,128]{2,1,0:T(8,128)(2,1)S(1)}, bf16[1,2880,128]{2,1,0:T(8,128)(2,1)}, u32[]{:S(2)}) copy-start(bf16[1,2880,128]{2,1,0:T(8,128)(2,1)} %param.23) | copy-start | bytes 2211844
  408.7 5.7 %copy-start.6 = (s32[192,4]{0,1:T(4,128)S(1)}, s32[192,4]{0,1:T(4,128)}, u32[]{:S(2)}) copy-start(s32[192,4]{0,1:T(4,128)} %param.20) | copy-start | bytes 9220
  408.7 50.9 %all-to-all-start.2 = ((bf16[8,160,720]{2,1,0:T(8,128)(2,1)}), bf16[8,160,720]{2,1,0:T(8,128)(2,1)S(1)}, u32[]{:S(2)}, u32[]{:S(2)}) async-start(bf16[8,160,720]{2,1,0:T(8,128)(2,1)} %copy.47), calls=%async_computation.2 | async-start | bytes 3932160 | tf_op jit(solution)/shard_map/all_to_all | solution.py:129
  468.2 7.7 %copy-start.1 = (bf16[512,2880]{0,1:T(8,128)(2,1)S(1)}, bf16[512,2880]{0,1:T(8,128)(2,1)}, u32[]{:S(2)}) copy-start(bf16[512,2880]{0,1:T(8,128)(2,1)} %param.17) | copy-start | bytes 8847364
Sparse Core Ops, SparseCore 0:
  21.8 29.1 reduce-scatter.6
  53.1 17.4 all-gather.2
  335.5 64.2 reduce-scatter.8
where the time goes:
time: 484 us; the launch traced here: 482 us
  waiting for transfers between devices  298 us (62%)
  local copies, waits for them, and re-layouts  104 us (21%)
  matrix products  34.6 us (7%)
  starting transfers between devices  22.1 us (5%)
  between operations  14 us (3%)
  other arithmetic  9.88 us (2%)
    all_to_all x1, waiting for transfers between devices, shards(): lax.all_to_all(sent_rows, 'ex', split_axis=0, concat_axis=0, tiled=True)  159 us
    unnamed x5, waiting for transfers between devices  93.7 us
    unnamed x29, local copies, waits for them, and re-layouts  56.1 us
    all_to_all x1, waiting for transfers between devices, shards(): lax.all_to_all(shares.astype(jnp.bfloat16), 'ex', split_axis=0, concat_ax...  45.1 us
    dot_general x1, matrix products, shards(): jnp.dot(slot_rows, gate_up[0].reshape(width, 2 * hidden_here), preferred_...  11.2 us
    convert_element_type x1, local copies, waits for them, and re-layouts, shards(): jnp.dot(activated, down_proj[0], preferred_element_type=jnp.float32)  10.4 us
    gather x2, local copies, waits for them, and re-layouts, shards(): picked = returned.reshape(experts_all * capacity, columns)[target]  10 us
    dot_general x1, matrix products, shards(): jnp.dot(activated, down_proj[0], preferred_element_type=jnp.float32)  9.87 us
  transfers between devices with their start and end apart: 7, of which 4 were waited for; matrix products, arithmetic and copies ran while one was open for 7% of the time, Pallas kernels for 0%

commit v1 on v0

--- a/solution.py
+++ b/solution.py
@@ -37,6 +37,7 @@
     group_size = heads_here // kv_here
     head_size = keys_values.shape[2] // 2
     rim_rows = WINDOW - 1
+    table = token_table(routes, route_scores, tenants, gate_up.shape[0] * lax.axis_size("ex"))
     before = from_behind(keys_values[tok_rows - rim_rows :], "ex", 1)
     extended = jnp.concatenate([before, keys_values], axis=0)
     keys_only = extended[:, :, :head_size]
@@ -64,6 +65,91 @@
         head_terms.astype(jnp.bfloat16), "tp", scatter_dimension=1, tiled=True
     ).astype(jnp.float32)
     residual_out = (residual_in.astype(jnp.float32) + head_share).astype(jnp.bfloat16)
+    sources = lax.axis_size("ex")
+    experts_all = gate_up.shape[0] * sources
+    capacity = 5 * tok_rows * TOP // (3 * experts_all)
+    if gate_up.shape[0] == 1 and 2 * capacity >= tok_rows:
+        mixed = dense_experts(
+            residual_out, table, norm_gain, gate_up, adapter_in, adapter_out, down_proj
+        )
+        return (residual_out, mixed)
+    return (
+        residual_out,
+        routed_experts(
+            residual_out, norm_gain, routes, route_scores, tenants,
+            gate_up, adapter_in, adapter_out, down_proj, columns,
+        ),
+    )
+
+
+def token_table(routes, route_scores, tenants, experts_all):
+    score_float = route_scores.astype(jnp.float32)
+    share = score_float / jnp.sum(score_float, axis=1, keepdims=True)
+    hit = routes[:, :, None] == jnp.arange(experts_all, dtype=jnp.int32)[None, None, :]
+    by_expert = jnp.sum(jnp.where(hit, share[:, :, None], 0.0), axis=1)
+    return jnp.concatenate([by_expert, tenants.astype(jnp.float32)[:, None]], axis=1)
+
+
+def dense_experts(
+    residual_out, table, norm_gain, gate_up, adapter_in, adapter_out, down_proj
+):
+    tok_rows, columns = residual_out.shape
+    sources = lax.axis_size("ex")
+    quarters = lax.axis_size("tp")
+    width = columns * quarters
+    rows_all = sources * tok_rows
+    hidden_here = gate_up.shape[3]
+    rank_cols = adapter_in.shape[2]
+    tokens = gather_tokens(residual_out)
+    whole_rows = tokens.astype(jnp.float32)
+    inverse = lax.rsqrt(jnp.mean(whole_rows * whole_rows, axis=-1, keepdims=True) + 1e-05)
+    normed = (whole_rows * inverse * norm_gain).astype(jnp.bfloat16)
+    everyone = lax.all_gather(table, "ex", axis=0, tiled=True)
+    expert = lax.axis_index("ex")
+    here = jnp.arange(everyone.shape[1], dtype=jnp.int32)[None, :] == expert
+    weight = jnp.sum(jnp.where(here, everyone, 0.0), axis=1, keepdims=True)
+    tenant = everyone[:, -1:].astype(jnp.int32)
+    mapped = jnp.dot(
+        normed, gate_up[0].reshape(width, 2 * hidden_here), preferred_element_type=jnp.float32
+    )
+    low_rank = jnp.dot(normed, adapter_in[0], preferred_element_type=jnp.float32)
+    keep = (jnp.arange(rank_cols, dtype=jnp.int32) // RANK)[None, :] == tenant
+    low_rank = jnp.where(keep, low_rank, 0.0).astype(jnp.bfloat16)
+    mapped = mapped + jnp.dot(
+        low_rank,
+        adapter_out[0].reshape(rank_cols, 2 * hidden_here),
+        preferred_element_type=jnp.float32,
+    )
+    gate_part = mapped[:, :hidden_here]
+    up_part = mapped[:, hidden_here:]
+    activated = (
+        gate_part * jax.nn.sigmoid(1.702 * gate_part) * (up_part + 1.0) * weight
+    ).astype(jnp.bfloat16)
+    terms = jnp.dot(activated, down_proj[0], preferred_element_type=jnp.float32).astype(
+        jnp.bfloat16
+    )
+    return scatter_terms(terms)
+
+
+def gather_tokens(residual_out):
+    tok_rows, columns = residual_out.shape
+    sources, quarters = lax.axis_size("ex"), lax.axis_size("tp")
+    blocks = lax.all_gather(residual_out, ("ex", "tp"), axis=0, tiled=False)
+    blocks = blocks.reshape(sources, quarters, tok_rows, columns).transpose(0, 2, 1, 3)
+    return blocks.reshape(sources * tok_rows, quarters * columns)
+
+
+def scatter_terms(terms):
+    mine = lax.psum_scatter(terms, "tp", scatter_dimension=1, tiled=True)
+    return lax.psum_scatter(mine, "ex", scatter_dimension=0, tiled=True)
+
+
+def routed_experts(
+    residual_out, norm_gain, routes, route_scores, tenants,
+    gate_up, adapter_in, adapter_out, down_proj, columns,
+):
+    tok_rows = residual_out.shape[0]
+    width = gate_up.shape[1]
     whole_rows = lax.all_gather(residual_out, "tp", axis=1, tiled=True).astype(jnp.float32)
     inverse = lax.rsqrt(jnp.mean(whole_rows * whole_rows, axis=-1, keepdims=True) + 1e-05)
     normed = (whole_rows * inverse * norm_gain).astype(jnp.bfloat16)
@@ -131,7 +217,7 @@
     ).astype(shares.dtype)
     picked = returned.reshape(experts_all * capacity, columns)[target]
     expert_mix = jnp.sum((picked * route_weight[:, None]).reshape(tok_rows, TOP, columns), axis=1)
-    return (residual_out, expert_mix.astype(jnp.bfloat16))
+    return expert_mix.astype(jnp.bfloat16)
 
 
 def solution(mesh):

time: 484 us -> 386 us (0.80)
  waiting for transfers between devices: 298 us -> 219 us
  local copies, waits for them, and re-layouts: 104 us -> 33.9 us
  other arithmetic: 9.88 us -> 43.4 us
  blocking collectives: 0 us -> 31.1 us
  starting transfers between devices: 22.1 us -> 5.06 us
    all_to_all x3 -> x0, waiting for transfers between devices: 204 us -> none  [the longest x1 159 us: shards(): lax.all_to_all(sent_rows, 'ex', split_axis=0, concat_axis=0, tiled=True)]
    reduce_scatter x0 -> x1, waiting for transfers between devices: none -> 72.8 us  [scatter_terms(): mine = lax.psum_scatter(terms, 'tp', scatter_dimension=1, tiled=True)]
    all_gather x1, waiting for transfers between devices: 0.01 us -> 46.3 us  [gather_tokens(): blocks = lax.all_gather(residual_out, ('ex', 'tp'), axis=0, tiled=False)]
    unnamed x29 -> x26, local copies, waits for them, and re-layouts: 56.1 us -> 15.3 us
    convert_element_type x2 -> x4, other arithmetic: 0.27 us -> 36.5 us  [the longest x1 23.8 us: dense_experts(): normed = (whole_rows * inverse * norm_gain).astype(jnp.bfloat16)]
    all_gather x0 -> x1, blocking collectives: none -> 31.1 us  [dense_experts(): everyone = lax.all_gather(table, 'ex', axis=0, tiled=True)]
    gather x4 -> x0, local copies, waits for them, and re-layouts: 25 us -> none  [the longest x2 10 us: shards(): picked = returned.reshape(experts_all * capacity, columns)[target]]
    all_to_all x3 -> x0, starting transfers between devices: 17.1 us -> none  [the longest x1 5.98 us: shards(): lax.all_to_all(sent_rows, 'ex', split_axis=0, concat_axis=0, tiled=True)]
  transfers between devices with their start and end apart: 7 -> 5, of which waited for: 4 -> 4; matrix products, arithmetic and copies ran while one was open for 7% -> 2% of each run, Pallas kernels for 0% -> 0%
where the time goes in v1:
time: 386 us; the launch traced here: 385 us
  waiting for transfers between devices  219 us (57%)
  other arithmetic  43.4 us (11%)
  matrix products  39.4 us (10%)
  local copies, waits for them, and re-layouts  33.9 us (9%)
  blocking collectives  31.1 us (8%)
  between operations  14 us (4%)
  starting transfers between devices  5.06 us (1%)
    unnamed x6, waiting for transfers between devices  99.4 us
    reduce_scatter x1, waiting for transfers between devices, scatter_terms(): mine = lax.psum_scatter(terms, 'tp', scatter_dimension=1, tiled=True)  72.8 us
    all_gather x1, waiting for transfers between devices, gather_tokens(): blocks = lax.all_gather(residual_out, ('ex', 'tp'), axis=0, tiled=False)  46.3 us
    all_gather x1, blocking collectives, dense_experts(): everyone = lax.all_gather(table, 'ex', axis=0, tiled=True)  31.1 us
    convert_element_type x1, other arithmetic, dense_experts(): normed = (whole_rows * inverse * norm_gain).astype(jnp.bfloat16)  23.8 us
    convert_element_type x1, local copies, waits for them, and re-layouts, dense_experts(): normed = (whole_rows * inverse * norm_gain).astype(jnp.bfloat16)  17.7 us
    unnamed x26, local copies, waits for them, and re-layouts  15.3 us
    dot_general x1, matrix products, dense_experts(): jnp.dot(normed, gate_up[0].reshape(width, 2 * hidden_here), preferred_ele...  12.8 us
  transfers between devices with their start and end apart: 5, of which 4 were waited for; matrix products, arithmetic and copies ran while one was open for 2% of the time, Pallas kernels for 0%

profile of v1, /device:TPU:0, one launch (start us, length us, event | category | flops | bytes accessed | tf_op | source)
XLA Modules:
  0.0 385.4 jit_solution(12304677267419445353)
XLA Ops:
  7.2 0.0 copy-start
  7.2 0.0 reduce-scatter.10.cloned.1.call-start
  7.2 1.0 copy.43
  8.3 0.1 slice.24
  8.4 4.9 %collective-permute-start = (bf16[127,1,128]{0,2,1:T(8,128)(2,1)S(1)}, bf16[127,1,128]{0,2,1:T(8,128)(2,1)S(1)}, u32[]{:S(2)}, u32[]{:S(2)}) collective-permute-start(bf16[127,1,128]{0,2,1:T(8,128)(2,1)S(1)} %slice.24), channel_id=1, source_target_pairs={{0,4},{4,8},{8,12},{12,16},{16,20},{20,24},{24,28},{1,5},{5,9},{9,... | collective-permute-start | bytes 97544 | tf_op jit(solution)/shard_map/ppermute | solution.py:14
  13.3 0.1 fusion.21
  13.5 1.1 copy.45
  14.5 0.7 exp.19
  15.2 0.0 collective-permute-done
  15.2 0.9 fusion.8
  16.1 0.1 broadcast_add_fusion
  16.2 0.8 convolution_convert_fusion.2
  17.0 0.0 copy-done
  17.0 2.1 convolution_convert_fusion.1
  19.2 2.5 copy.49
  21.7 0.0 reduce-scatter.10.cloned.1.call-update
  21.7 0.0 all-gather.4.cloned.1.call-start
  21.8 29.2 %reduce-scatter.10.cloned.1.call-done = bf16[720,192]{1,0:T(8,128)(2,1)} async-done(((bf16[2880,192]{1,0:T(8,128)(2,1)}), bf16[720,192]{1,0:T(8,128)(2,1)}) %reduce-scatter.10.cloned.1.call-update) | async-done | bytes 276496
  51.0 1.1 copy.50
  52.1 0.8 add_convert_fusion
  52.9 0.0 all-gather.4.cloned.1.call-update
  52.9 0.0 reduce-scatter.8.cloned.1.call-start
  53.0 0.1 mul.66
  53.1 0.0 copy-start.5
  53.1 0.0 copy-start.7
  53.1 0.0 copy-start.4
  53.1 5.2 %copy.53 = bf16[360,8,2,384]{3,1,2,0:T(8,128)(2,1)} copy(bf16[360,8,2,384]{3,2,1,0:T(2,128)(2,1)} %bitcast.65) | data formatting | bytes 8847360
  58.3 0.0 copy-done.8
  58.4 31.1 %all-gather.1 = f32[8,192,9]{1,2,0:T(8,128)S(1)} all-gather(f32[1,192,9]{1,2,0:T(8,128)S(1)} %maximum_bitcast_fusion), channel_id=1, replica_groups=mesh['ex'=8,'tp'=4] {'ex'}, dimensions={0}, use_global_device_ids=true | all-gather | bytes 62208 | tf_op jit(solution)/shard_map/all_gather | solution.py:107
  89.5 0.1 reshape.136
  89.7 0.1 select_reduce_fusion
  89.8 46.3 %all-gather.4.cloned.1.call-done = bf16[6144,720]{1,0:T(8,128)(2,1)} async-done(((bf16[192,720]{1,0:T(8,128)(2,1)}), bf16[6144,720]{1,0:T(8,128)(2,1)}) %all-gather.4.cloned.1.call-update) | async-done | bytes 8847376 | tf_op jit(solution)/shard_map/all_gather | solution.py:137
  136.1 12.6 %convert.1 = f32[8,4,192,720]{3,2,1,0:T(8,128)} convert(bf16[8,4,192,720]{3,2,1,0:T(8,128)(2,1)} %bitcast.62) | non-fusion elementwise | flops 4423680 | bytes 26542080 | tf_op jit(solution)/shard_map/convert_element_type | solution.py:104
  148.7 5.8 %multiply_reduce_fusion = f32[8,192]{1,0:T(8,128)S(1)} fusion(bf16[8,4,192,720]{3,2,1,0:T(8,128)(2,1)} %bitcast.63), kind=kLoop, calls=%fused_computation.3 | loop fusion | flops 13269504 | bytes 8853504 | tf_op jit(solution)/shard_map/reduce_sum | solution.py:105
  154.5 23.8 %fusion.2 = bf16[8,192,4,720]{3,2,1,0:T(4,128)(2,1)} fusion(f32[8,4,192,720]{3,2,1,0:T(8,128)} %convert.1, f32[4,720]{1,0:T(4,128)S(1)} %mul.66, f32[8,192]{1,0:T(8,128)S(1)} %add_rsqrt_fusion), kind=kLoop, calls=%fused_computation.5 | loop fusion | flops 13271040 | bytes 26559744 | tf_op jit(solution)/shard_map/convert_element_type | solution.py:106
  178.3 17.7 %convert_element_type.74 = bf16[1536,2880]{1,0:T(8,128)(2,1)} reshape(bf16[8,192,4,720]{3,2,1,0:T(4,128)(2,1)} %fusion.2) | data formatting | bytes 17694720 | tf_op jit(solution)/shard_map/convert_element_type | solution.py:106
  196.1 12.8 %fusion.37 = f32[1536,768]{1,0:T(8,128)} fusion(bf16[1536,2880]{1,0:T(8,128)(2,1)} %convert_element_type.74, bf16[2880,768]{1,0:T(8,128)(2,1)} %bitcast.66), kind=kOutput, calls=%fused_computation.66 | convolution fusion | flops 6794772480 | bytes 17989632 | tf_op jit(solution)/shard_map/dot_general | solution.py:112
  208.9 0.0 copy-done.2
  208.9 11.2 %convolution_add_fusion = f32[1536,768]{1,0:T(8,128)} fusion(f32[1536,768]{1,0:T(8,128)} %fusion.37, bf16[128,768]{1,0:T(8,128)(2,1)S(1)} %bitcast.67, bf16[1536,2880]{1,0:T(8,128)(2,1)} %convert_element_type.74, bf16[1,2880,128]{2,1,0:T(8,128)(2,1)S(1)} %copy-done.2, s32[128]{0:T(128)S(1)} %and_select_fusion, s32[1536]{0:T(1024)S(1)} %fusion.29), kind=kOutput, calls=%fused_computation.6 | convolution fusion | flops 1436221440 | bytes 19225088 | tf_op jit(solution)/shard_map/dot_general | solution.py:118
  220.1 11.5 %convolution_convert_fusion = bf16[1536,2880]{0,1:T(8,128)(2,1)} fusion(bf16[1,384,2880]{1,2,0:T(8,128)(2,1)} %param.25, f32[1536,768]{1,0:T(8,128)} %convolution_add_fusion, f32[1536]{0:T(1024)S(1)} %select_reduce_fusion), kind=kOutput, calls=%fused_computation.4 | convolution fusion | flops 3407118336 | bytes 15783936 | tf_op jit(solution)/shard_map/dot_general | solution.py:128
  231.6 0.0 reduce-scatter.8.cloned.1.call-update
  231.6 0.0 copy-start.1
  231.6 0.0 reduce-scatter.12.cloned.1.call-start
  231.6 72.8 %reduce-scatter.8.cloned.1.call-done = bf16[1536,720]{0,1:T(8,128)(2,1)} async-done(((bf16[1536,2880]{0,1:T(8,128)(2,1)}), bf16[1536,720]{0,1:T(8,128)(2,1)}) %reduce-scatter.8.cloned.1.call-update) | async-done | bytes 2211856 | tf_op jit(solution)/shard_map/reduce_scatter | solution.py:143
  304.5 4.2 %copy.51 = bf16[1536,720]{1,0:T(8,128)(2,1)} copy(bf16[1536,720]{0,1:T(8,128)(2,1)} %reduce-scatter.8.cloned.1.call-done) | data formatting | bytes 4423680
  308.7 0.0 reduce-scatter.12.cloned.1.call-update
  308.7 70.1 %reduce-scatter.12.cloned.1.call-done = bf16[192,720]{1,0:T(8,128)(2,1)} async-done(((bf16[1536,720]{1,0:T(8,128)(2,1)}), bf16[192,720]{1,0:T(8,128)(2,1)}) %reduce-scatter.12.cloned.1.call-update) | async-done | bytes 276496
  378.8 0.0 copy-done.1
  (23 shorter events, 0.2 us)
Async XLA Ops:
  7.2 9.9 %copy-start = (bf16[512,2880]{0,1:T(8,128)(2,1)S(1)}, bf16[512,2880]{0,1:T(8,128)(2,1)}, u32[]{:S(2)}) copy-start(bf16[512,2880]{0,1:T(8,128)(2,1)} %param.17) | copy-start | bytes 8847364
  7.2 43.8 %reduce-scatter.10.cloned.1.call-start = ((), (), s32[]{:S(2)}) async-start(), calls=%async_computation.5 | async-start | bytes 1843200
  8.4 6.8 %collective-permute-start = (bf16[127,1,128]{0,2,1:T(8,128)(2,1)S(1)}, bf16[127,1,128]{0,2,1:T(8,128)(2,1)S(1)}, u32[]{:S(2)}, u32[]{:S(2)}) collective-permute-start(bf16[127,1,128]{0,2,1:T(8,128)(2,1)S(1)} %slice.24), channel_id=1, source_target_pairs={{0,4},{4,8},{8,12},{12,16},{16,20},{20,24},{24,28},{1,5},{5,9},{9,... | collective-permute-start | bytes 97544 | tf_op jit(solution)/shard_map/ppermute | solution.py:14
  19.1 33.0 %copy-start.3 = (bf16[192,720]{1,0:T(8,128)(2,1)S(1)}, bf16[192,720]{1,0:T(8,128)(2,1)}, u32[]{:S(2)}) copy-start(bf16[192,720]{1,0:T(8,128)(2,1)} %param.13) | copy-start | bytes 829444
  19.2 33.8 %copy-start.6 = (f32[2880]{0:T(1024)S(1)}, f32[2880]{0:T(1024)}, u32[]{:S(2)}) copy-start(f32[2880]{0:T(1024)} %param.18) | copy-start | bytes 34564
  21.7 114.4 %all-gather.4.cloned.1.call-start = ((), (), s32[]{:S(2)}) async-start(), calls=%async_computation.4 | async-start | bytes 9732096 | tf_op jit(solution)/shard_map/all_gather | solution.py:137
  52.9 251.6 %reduce-scatter.8.cloned.1.call-start = ((), (), s32[]{:S(2)}) async-start(), calls=%async_computation.3 | async-start | bytes 11059200 | tf_op jit(solution)/shard_map/reduce_scatter | solution.py:143
  53.1 5.2 %copy-start.8 = (s32[192]{0:T(256)S(1)}, s32[192]{0:T(256)}, u32[]{:S(2)}) copy-start(s32[192]{0:T(256)} %param.21) | copy-start | bytes 2308
  53.1 5.2 %copy-start.5 = (s32[192,4]{0,1:T(4,128)S(1)}, s32[192,4]{0,1:T(4,128)}, u32[]{:S(2)}) copy-start(s32[192,4]{0,1:T(4,128)} %param.20) | copy-start | bytes 9220
  53.1 5.2 %copy-start.7 = (s32[192,4]{0,1:T(4,128)S(1)}, s32[192,4]{0,1:T(4,128)}, u32[]{:S(2)}) copy-start(s32[192,4]{0,1:T(4,128)} %param.19) | copy-start | bytes 9220
  53.1 36.5 %copy-start.4 = (bf16[1,128,2,384]{3,2,1,0:T(2,128)(2,1)S(1)}, bf16[1,128,2,384]{3,2,1,0:T(2,128)(2,1)}, u32[]{:S(2)}) copy-start(bf16[1,128,2,384]{3,2,1,0:T(2,128)(2,1)} %param.24) | copy-start | bytes 589828
  196.1 12.8 %copy-start.2 = (bf16[1,2880,128]{2,1,0:T(8,128)(2,1)S(1)}, bf16[1,2880,128]{2,1,0:T(8,128)(2,1)}, u32[]{:S(2)}) copy-start(bf16[1,2880,128]{2,1,0:T(8,128)(2,1)} %param.23) | copy-start | bytes 2211844
  231.6 147.2 %copy-start.1 = (bf16[512,2880]{0,1:T(8,128)(2,1)S(1)}, bf16[512,2880]{0,1:T(8,128)(2,1)}, u32[]{:S(2)}) copy-start(bf16[512,2880]{0,1:T(8,128)(2,1)} %param.17) | copy-start | bytes 8847364
  231.6 147.2 %reduce-scatter.12.cloned.1.call-start = ((), (), s32[]{:S(2)}) async-start(), calls=%async_computation.6 | async-start | bytes 2654208
Sparse Core Ops, SparseCore 0:
  21.8 29.1 reduce-scatter.9
  54.4 81.6 all-gather.3
  231.7 72.7 reduce-scatter.7
  308.9 69.9 reduce-scatter.11

commit v2 on v0

--- a/solution.py
+++ b/solution.py
@@ -1,6 +1,10 @@
+import functools
+
 import jax
 import jax.numpy as jnp
 from jax import lax
+from jax.experimental import pallas as pl
+from jax.experimental.pallas import tpu as pltpu
 from jax.sharding import PartitionSpec as P
 
 WINDOW = 128
@@ -64,6 +68,313 @@
         head_terms.astype(jnp.bfloat16), "tp", scatter_dimension=1, tiled=True
     ).astype(jnp.float32)
     residual_out = (residual_in.astype(jnp.float32) + head_share).astype(jnp.bfloat16)
+    sources = lax.axis_size("ex")
+    experts_all = gate_up.shape[0] * sources
+    capacity = 5 * tok_rows * TOP // (3 * experts_all)
+    grouped = lax.axis_size("tp") == 4 and sources % 2 == 0
+    if grouped and gate_up.shape[0] == 1 and 2 * capacity >= tok_rows and experts_all <= 256:
+        mixed = dense_experts(
+            residual_out, routes, route_scores, tenants,
+            norm_gain, gate_up, adapter_in, adapter_out, down_proj,
+        )
+        return (residual_out, mixed)
+    return (
+        residual_out,
+        routed_experts(
+            residual_out, norm_gain, routes, route_scores, tenants,
+            gate_up, adapter_in, adapter_out, down_proj, columns,
+        ),
+    )
+
+
+MESH = pl.DeviceIdType.MESH
+
+
+def place():
+    ex, tp = lax.axis_index("ex"), lax.axis_index("tp")
+    return ex // 2, ex % 2, tp // 2, tp % 2
+
+
+def device(z, y, x, c):
+    return (z * 2 + y, x * 2 + c)
+
+
+def meet(peers):
+    barrier = pltpu.get_barrier_semaphore()
+    for peer in peers:
+        pl.semaphore_signal(barrier, inc=1, device_id=peer, device_id_type=MESH)
+    pl.semaphore_wait(barrier, len(peers))
+
+
+def gather_kernel(
+    deep, mine, out, own_sem, z_send, z_recv, x_send, x_recv, y_send, y_recv,
+    dx_send, dx_recv, dy_send, dy_recv, c_send, c_recv,
+):
+    z, y, x, c = place()
+    half = mine.shape[0] // 2
+    first, second = pl.ds(0, half), pl.ds(half, half)
+    at_x, at_y, at_c = device(z, y, 1 - x, c), device(z, 1 - y, x, c), device(z, y, x, 1 - c)
+    meet(
+        [device(lax.rem(z + k, deep), y, x, c) for k in range(1, deep)] + [at_x, at_y, at_c]
+    )
+
+    def send(src, dst, sems, number, to):
+        copy = pltpu.make_async_remote_copy(
+            src_ref=src, dst_ref=dst, send_sem=sems[0].at[number], recv_sem=sems[1].at[number],
+            device_id=to, device_id_type=MESH,
+        )
+        copy.start()
+        return copy
+
+    def whole(k, yy, xx, cc):
+        return out.at[lax.rem(z - k + deep, deep), yy, xx, cc]
+
+    own = pltpu.make_async_copy(mine, whole(0, y, x, c), own_sem)
+    own.start()
+    z_sems, x_sems, y_sems = (z_send, z_recv), (x_send, x_recv), (y_send, y_recv)
+    dx_sems, dy_sems, c_sems = (dx_send, dx_recv), (dy_send, dy_recv), (c_send, c_recv)
+    sent = []
+    down = [None]
+    for k in range(1, deep):
+        copy = send(mine, whole(0, y, x, c), z_sems, k, device(lax.rem(z + k, deep), y, x, c))
+        down.append(copy)
+        sent.append(copy)
+    to_x, to_y, to_c = [], [], []
+    for k in range(deep):
+        slot = whole(k, y, x, c)
+        if k:
+            down[k].wait_recv()
+        src = slot if k else mine
+        to_x.append(send(src, slot, x_sems, k, at_x))
+        to_y.append(send(src, slot, y_sems, k, at_y))
+        to_c.append(send(src, slot, c_sems, k, at_c))
+    cross_x, cross_y = [], []
+    for k in range(deep):
+        slot = whole(k, 1 - y, x, c)
+        to_y[k].wait_recv()
+        cross_x.append(send(slot.at[first], slot.at[first], dx_sems, k, at_x))
+        to_c.append(send(slot, slot, c_sems, deep + 2 * k, at_c))
+        slot = whole(k, y, 1 - x, c)
+        to_x[k].wait_recv()
+        cross_y.append(send(slot.at[second], slot.at[second], dy_sems, k, at_y))
+        to_c.append(send(slot, slot, c_sems, deep + 2 * k + 1, at_c))
+    for k in range(deep):
+        slot = whole(k, 1 - y, 1 - x, c)
+        cross_x[k].wait_recv()
+        to_c.append(send(slot.at[first], slot.at[first], c_sems, 3 * deep + 2 * k, at_c))
+        cross_y[k].wait_recv()
+        to_c.append(send(slot.at[second], slot.at[second], c_sems, 3 * deep + 2 * k + 1, at_c))
+    own.wait()
+    for copy in to_c:
+        copy.wait_recv()
+    for copy in sent + to_x + to_y + cross_x + cross_y + to_c:
+        copy.wait_send()
+
+
+def gather_rows(block):
+    deep = lax.axis_size("ex") // 2
+    dma = pltpu.SemaphoreType.DMA
+    return pl.pallas_call(
+        functools.partial(gather_kernel, deep),
+        out_shape=jax.ShapeDtypeStruct((deep, 2, 2, 2) + block.shape, block.dtype),
+        in_specs=[pl.BlockSpec(memory_space=pltpu.VMEM)],
+        out_specs=pl.BlockSpec(memory_space=pl.ANY),
+        scratch_shapes=[dma] + [dma((deep,))] * 10 + [dma((5 * deep,))] * 2,
+        compiler_params=pltpu.CompilerParams(collective_id=0, has_side_effects=True),
+    )(block)
+
+
+def scatter_kernel(
+    deep, terms, out, part, core_in, dx_in, dy_in, x_in, y_in, z_in, c_send, c_recv,
+    dx_send, dx_recv, dy_send, dy_recv, x_send, x_recv, y_send, y_recv, z_send, z_recv,
+):
+    z, y, x, c = place()
+    half = out.shape[0] // 2
+    first, second = pl.ds(0, half), pl.ds(half, half)
+    at_x, at_y, at_c = device(z, y, 1 - x, c), device(z, 1 - y, x, c), device(z, y, x, 1 - c)
+    meet(
+        [device(lax.rem(z + k, deep), y, x, c) for k in range(1, deep)] + [at_x, at_y, at_c]
+    )
+
+    def send(src, dst, sems, number, to):
+        copy = pltpu.make_async_remote_copy(
+            src_ref=src, dst_ref=dst, send_sem=sems[0].at[number], recv_sem=sems[1].at[number],
+            device_id=to, device_id_type=MESH,
+        )
+        copy.start()
+        return copy
+
+    def wide(value):
+        return value.astype(jnp.float32)
+
+    z_sems, x_sems, y_sems = (z_send, z_recv), (x_send, x_recv), (y_send, y_recv)
+    dx_sems, dy_sems, c_sems = (dx_send, dx_recv), (dy_send, dy_recv), (c_send, c_recv)
+    corners = ((1 - y, 1 - x), (1 - y, x), (y, 1 - x), (y, x))
+
+    def far(k):
+        return lax.rem(z + deep - 1 - k, deep)
+
+    on_chip = []
+    for group, (yy, xx) in enumerate(corners):
+        for k in range(deep):
+            number = group * deep + k
+            on_chip.append(
+                send(terms.at[far(k), yy, xx, 1 - c], core_in.at[number], c_sems, number, at_c)
+            )
+
+    def add_core(group, k):
+        yy, xx = corners[group]
+        number = group * deep + k
+        on_chip[number].wait_recv()
+        part[number] = (
+            wide(terms[far(k), yy, xx, c]) + wide(core_in[number])
+        ).astype(part.dtype)
+
+    sent = list(on_chip)
+    cross_x, cross_y, to_x, to_y, to_z = [], [], [], [], []
+    for k in range(deep):
+        add_core(0, k)
+        cross_x.append(send(part.at[k, first], dx_in.at[k], dx_sems, k, at_x))
+        cross_y.append(send(part.at[k, second], dy_in.at[k], dy_sems, k, at_y))
+    for k in range(deep):
+        add_core(1, k)
+        add_core(2, k)
+        cross_x[k].wait_recv()
+        near = deep + k
+        part[near, first] = (wide(part[near, first]) + wide(dx_in[k])).astype(part.dtype)
+        to_y.append(send(part.at[near], y_in.at[k], y_sems, k, at_y))
+        cross_y[k].wait_recv()
+        near = 2 * deep + k
+        part[near, second] = (wide(part[near, second]) + wide(dy_in[k])).astype(part.dtype)
+        to_x.append(send(part.at[near], x_in.at[k], x_sems, k, at_x))
+    for k in range(deep):
+        add_core(3, k)
+        near = 3 * deep + k
+        to_x[k].wait_recv()
+        to_y[k].wait_recv()
+        part[near] = (wide(part[near]) + wide(x_in[k]) + wide(y_in[k])).astype(part.dtype)
+        if k < deep - 1:
+            to_z.append(
+                send(part.at[near], z_in.at[k], z_sems, k, device(far(k), y, x, c))
+            )
+    total = wide(part[4 * deep - 1])
+    for k in range(deep - 1):
+        to_z[k].wait_recv()
+        total = total + wide(z_in[k])
+    out[...] = total.astype(out.dtype)
+    for copy in sent + cross_x + cross_y + to_x + to_y + to_z:
+        copy.wait_send()
+
+
+def scatter_terms(terms):
+    deep = lax.axis_size("ex") // 2
+    rows, columns = terms.shape[-2:]
+    dma = pltpu.SemaphoreType.DMA
+
+    def slots(count, size):
+        return pltpu.VMEM((count, size, columns), terms.dtype)
+
+    return pl.pallas_call(
+        functools.partial(scatter_kernel, deep),
+        out_shape=jax.ShapeDtypeStruct((rows, columns), terms.dtype),
+        in_specs=[pl.BlockSpec(memory_space=pltpu.VMEM)],
+        out_specs=pl.BlockSpec(memory_space=pltpu.VMEM),
+        scratch_shapes=[
+            slots(4 * deep, rows), slots(4 * deep, rows), slots(deep, rows // 2),
+            slots(deep, rows // 2), slots(deep, rows), slots(deep, rows), slots(deep, rows),
+        ]
+        + [dma((4 * deep,))] * 2
+        + [dma((deep,))] * 10,
+        compiler_params=pltpu.CompilerParams(
+            collective_id=1, has_side_effects=True, vmem_limit_bytes=60 * 1024 * 1024
+        ),
+    )(terms.reshape((deep, 2, 2, 2) + terms.shape[-2:]))
+
+
+def expert_kernel(tokens, gain, weight_gu, weight_in, weight_out, weight_down, terms):
+    expert = lax.axis_index("ex")
+    held, quarters, tok_rows, padded = tokens.shape
+    columns = gain.shape[2]
+    rows = held * tok_rows
+    hidden = weight_down.shape[1]
+    rank_cols = weight_in.shape[2]
+
+    def quarter(q):
+        return tokens[:, q].reshape(rows, padded)
+
+    meta = quarter(0)[:, columns : columns + 2 * TOP + 1].astype(jnp.float32)
+    routes, scores, tenant = meta[:, :TOP], meta[:, TOP : 2 * TOP], meta[:, 2 * TOP :]
+    chosen = jnp.where(routes == expert.astype(jnp.float32), scores, 0.0)
+    weight = jnp.sum(chosen, axis=1, keepdims=True) / jnp.sum(scores, axis=1, keepdims=True)
+    squares = jnp.zeros((rows, 1), jnp.float32)
+    for q in range(quarters):
+        wide = quarter(q)[:, :columns].astype(jnp.float32)
+        squares += jnp.sum(wide * wide, axis=1, keepdims=True)
+    inverse = lax.rsqrt(squares / (quarters * columns) + 1e-05)
+    mapped = jnp.zeros((rows, 2 * hidden), jnp.float32)
+    low_rank = jnp.zeros((rows, rank_cols), jnp.float32)
+    for q in range(quarters):
+        wide = quarter(q)[:, :columns].astype(jnp.float32)
+        normed = (wide * inverse * gain[q]).astype(jnp.bfloat16)
+        mapped += jnp.dot(normed, weight_gu[q], preferred_element_type=jnp.float32)
+        low_rank += jnp.dot(normed, weight_in[q], preferred_element_type=jnp.float32)
+    owner = lax.broadcasted_iota(jnp.int32, (rows, rank_cols), 1) // RANK
+    low_rank = jnp.where(owner == tenant.astype(jnp.int32), low_rank, 0.0).astype(jnp.bfloat16)
+    mapped += jnp.dot(low_rank, weight_out[...], preferred_element_type=jnp.float32)
+    gate_part, up_part = mapped[:, :hidden], mapped[:, hidden:]
+    activated = gate_part * jax.nn.sigmoid(1.702 * gate_part) * (up_part + 1.0)
+    activated = (activated * weight).astype(jnp.bfloat16)
+    for q in range(quarters):
+        term = jnp.dot(activated, weight_down[q], preferred_element_type=jnp.float32)
+        terms[:, q] = term.astype(jnp.bfloat16).reshape(held, tok_rows, columns)
+
+
+def dense_experts(
+    residual_out, routes, route_scores, tenants,
+    norm_gain, gate_up, adapter_in, adapter_out, down_proj,
+):
+    tok_rows, columns = residual_out.shape
+    sources, quarters = lax.axis_size("ex"), lax.axis_size("tp")
+    hidden = gate_up.shape[3]
+    rank_cols = adapter_in.shape[2]
+    meta = jnp.concatenate([routes, route_scores, tenants[:, None]], axis=1).astype(jnp.bfloat16)
+    padded = -(-(columns + meta.shape[1]) // 128) * 128
+    fill = jnp.zeros((tok_rows, padded - columns - meta.shape[1]), jnp.bfloat16)
+    block = jnp.concatenate([residual_out, meta, fill], axis=1)
+    tokens = gather_rows(block).reshape(sources, quarters, tok_rows, padded)
+    step = 2
+    fixed = lambda *shape: pl.BlockSpec(shape, lambda i: (0,) * len(shape))
+    terms = pl.pallas_call(
+        expert_kernel,
+        grid=(sources // step,),
+        out_shape=jax.ShapeDtypeStruct((sources, quarters, tok_rows, columns), jnp.bfloat16),
+        in_specs=[
+            pl.BlockSpec((step, quarters, tok_rows, padded), lambda i: (i, 0, 0, 0)),
+            fixed(quarters, 1, columns),
+            fixed(quarters, columns, 2 * hidden),
+            fixed(quarters, columns, rank_cols),
+            fixed(rank_cols, 2 * hidden),
+            fixed(quarters, hidden, columns),
+        ],
+        out_specs=pl.BlockSpec((step, quarters, tok_rows, columns), lambda i: (i, 0, 0, 0)),
+        compiler_params=pltpu.CompilerParams(vmem_limit_bytes=60 * 1024 * 1024),
+    )(
+        tokens,
+        norm_gain.reshape(quarters, 1, columns),
+        gate_up[0].reshape(quarters, columns, 2 * hidden),
+        adapter_in[0].reshape(quarters, columns, rank_cols),
+        adapter_out[0].reshape(rank_cols, 2 * hidden),
+        down_proj[0].reshape(hidden, quarters, columns).transpose(1, 0, 2),
+    )
+    return scatter_terms(terms)
+
+
+def routed_experts(
+    residual_out, norm_gain, routes, route_scores, tenants,
+    gate_up, adapter_in, adapter_out, down_proj, columns,
+):
+    tok_rows = residual_out.shape[0]
+    width = gate_up.shape[1]
     whole_rows = lax.all_gather(residual_out, "tp", axis=1, tiled=True).astype(jnp.float32)
     inverse = lax.rsqrt(jnp.mean(whole_rows * whole_rows, axis=-1, keepdims=True) + 1e-05)
     normed = (whole_rows * inverse * norm_gain).astype(jnp.bfloat16)
@@ -131,7 +442,7 @@
     ).astype(shares.dtype)
     picked = returned.reshape(experts_all * capacity, columns)[target]
     expert_mix = jnp.sum((picked * route_weight[:, None]).reshape(tok_rows, TOP, columns), axis=1)
-    return (residual_out, expert_mix.astype(jnp.bfloat16))
+    return expert_mix.astype(jnp.bfloat16)
 
 
 def solution(mesh):

time: 484 us -> 204 us (0.42)
  waiting for transfers between devices: 298 us -> 10.8 us
  Pallas kernels: 0 us -> 140 us
  local copies, waits for them, and re-layouts: 104 us -> 28.6 us
  matrix products: 34.6 us -> 3.86 us
  starting transfers between devices: 22.1 us -> 4.94 us
  other arithmetic: 9.88 us -> 1.28 us
    all_to_all x3 -> x0, waiting for transfers between devices: 204 us -> none  [the longest x1 159 us: shards(): lax.all_to_all(sent_rows, 'ex', split_axis=0, concat_axis=0, tiled=True)]
    pallas_call x0 -> x3, Pallas kernels: none -> 140 us  [the longest x1 62 us: scatter_terms(): pl.pallas_call(functools.partial(scatter_kernel, deep), out_shape=jax.Sha...]
    unnamed x5 -> x2, waiting for transfers between devices: 93.7 us -> 10.8 us
    unnamed x29 -> x20, local copies, waits for them, and re-layouts: 56.1 us -> 8.36 us
    dot_general x3 -> x0, matrix products: 30.7 us -> none  [the longest x1 11.2 us: shards(): jnp.dot(slot_rows, gate_up[0].reshape(width, 2 * hidden_here), preferred_...]
    gather x4 -> x0, local copies, waits for them, and re-layouts: 25 us -> none  [the longest x2 10 us: shards(): picked = returned.reshape(experts_all * capacity, columns)[target]]
    all_to_all x3 -> x0, starting transfers between devices: 17.1 us -> none  [the longest x1 5.98 us: shards(): lax.all_to_all(sent_rows, 'ex', split_axis=0, concat_axis=0, tiled=True)]
    convert_element_type x3 -> x0, local copies, waits for them, and re-layouts: 17.1 us -> none  [the longest x1 10.4 us: shards(): jnp.dot(activated, down_proj[0], preferred_element_type=jnp.float32)]
  transfers between devices with their start and end apart: 7 -> 2, of which waited for: 4 -> 1; matrix products, arithmetic and copies ran while one was open for 7% -> 10% of each run, Pallas kernels for 0% -> 0%
where the time goes in v2:
time: 204 us
  Pallas kernels  140 us (69%)
  local copies, waits for them, and re-layouts  28.6 us (14%)
  between operations  14.2 us (7%)
  waiting for transfers between devices  10.8 us (5%)
  starting transfers between devices  4.94 us (2%)
  matrix products  3.86 us (2%)
    pallas_call x1, Pallas kernels, scatter_terms(): pl.pallas_call(functools.partial(scatter_kernel, deep), out_shape=jax.Sha...  62 us
    pallas_call x1, Pallas kernels, gather_rows(): pl.pallas_call(functools.partial(gather_kernel, deep), out_shape=jax.Shap...  53.7 us
    pallas_call x1, Pallas kernels, dense_experts(): pl.pallas_call(expert_kernel, grid=(sources // step,), out_shape=jax.Shap...  24.2 us
    unnamed x2, waiting for transfers between devices  10.8 us
    another operation x1, local copies, waits for them, and re-layouts, dense_experts(): gate_up[0].reshape(quarters, columns, 2 * hidden)  10.7 us
    unnamed x20, local copies, waits for them, and re-layouts  8.36 us
    ppermute x1, starting transfers between devices, from_behind(): lax.ppermute(value, axis, [(source, source + steps) for source in range(i...  4.9 us
    another operation x1, local copies, waits for them, and re-layouts, dense_experts(): down_proj[0].reshape(hidden, quarters, columns).transpose(1, 0, 2)  4.18 us
  transfers between devices with their start and end apart: 2, of which 1 were waited for; matrix products, arithmetic and copies ran while one was open for 10% of the time, Pallas kernels for 0%

profile of v2, /device:TPU:0, one launch (start us, length us, event | category | flops | bytes accessed | tf_op | source)
XLA Modules:
  0.0 203.5 jit_solution(17327394395015609133)
XLA Ops:
  7.2 0.0 copy-start
  7.2 0.0 reduce-scatter.4.cloned.1.call-start
  7.2 1.0 copy.27
  8.3 0.1 slice.12
  8.4 4.9 %collective-permute-start = (bf16[127,1,128]{0,2,1:T(8,128)(2,1)S(1)}, bf16[127,1,128]{0,2,1:T(8,128)(2,1)S(1)}, u32[]{:S(2)}, u32[]{:S(2)}) collective-permute-start(bf16[127,1,128]{0,2,1:T(8,128)(2,1)S(1)} %slice.12), channel_id=1, source_target_pairs={{0,4},{4,8},{8,12},{12,16},{16,20},{20,24},{24,28},{1,5},{5,9},{9,... | collective-permute-start | bytes 97544 | tf_op jit(solution)/shard_map/ppermute | solution.py:18
  13.3 0.1 fusion.3
  13.5 0.7 exp.16
  14.1 1.1 copy.29
  15.2 0.0 collective-permute-done
  15.2 0.9 fusion
  16.1 0.1 broadcast_add_fusion
  16.2 0.8 convolution_convert_fusion.1
  17.0 0.0 copy-done
  17.0 2.1 %convolution_convert_fusion = bf16[192,2880]{1,0:T(8,128)(2,1)} fusion(bf16[192,512]{0,1:T(8,128)(2,1)S(1)} %bitcast.51, bf16[512,2880]{0,1:T(8,128)(2,1)S(1)} %copy-done), kind=kOutput, calls=%fused_computation | convolution fusion | flops 566784000 | bytes 4251648 | tf_op jit(solution)/shard_map/dot_general | solution.py:66
  19.2 0.0 copy-start.6
  19.2 0.0 copy-start.4
  19.2 0.0 copy-start.5
  19.2 0.0 copy-start.3
  19.2 0.0 copy-start.2
  19.2 2.7 %copy.34 = bf16[192,2880]{0,1:T(8,128)(2,1)} copy(bf16[192,2880]{1,0:T(8,128)(2,1)} %convolution_convert_fusion) | data formatting | bytes 2211840
  21.9 0.0 reduce-scatter.4.cloned.1.call-update
  21.9 0.0 copy-done.6
  21.9 0.0 copy-done.4
  21.9 0.0 copy-done.5
  22.0 0.0 copy-done.3
  22.0 0.7 reshape.82.gain
  22.6 0.8 copy.31
  23.4 0.8 copy.30
  24.2 0.7 broadcast_in_dim.24
  24.9 0.0 copy-done.2
  24.9 0.7 copy.36
  25.6 4.2 %copy.33 = bf16[384,4,720]{2,0,1:T(8,128)(2,1)} copy(bf16[384,4,720]{0,2,1:T(8,128)(2,1)} %bitcast.47) | data formatting | bytes 4423680 | tf_op jit(solution)/shard_map/reshape;squeeze | solution.py:367
  29.7 10.7 %reshape_squeeze.12.weight_gu = bf16[4,720,768]{2,1,0:T(8,128)(2,1)} reshape(bf16[1,2880,2,384]{3,2,1,0:T(2,128)(2,1)} %param.22) | data formatting | bytes 8847360 | tf_op jit(solution)/shard_map/reshape;squeeze | solution.py:364
  40.4 10.7 %reduce-scatter.4.cloned.1.call-done = bf16[720,192]{1,0:T(8,128)(2,1)} async-done(((bf16[2880,192]{1,0:T(8,128)(2,1)}), bf16[720,192]{1,0:T(8,128)(2,1)}) %reduce-scatter.4.cloned.1.call-update) | async-done | bytes 276496
  51.1 1.1 copy.35
  52.3 1.0 add_convert_fusion
  53.3 0.0 copy-start.1
  53.3 1.8 concatenate.10.mine
  55.1 53.7 %shard_map.140 = bf16[4,2,2,2,192,768]{5,4,3,2,1,0:T(8,128)(2,1)} custom-call(bf16[192,768]{1,0:T(8,128)(2,1)} %concatenate.10.mine), custom_call_target="tpu_custom_call" | custom-call | tf_op jit(solution)/shard_map/pallas_call | solution.py:177
  108.8 0.0 copy-done.1
  108.8 24.2 %shard_map.141 = bf16[8,4,192,720]{3,2,1,0:T(8,128)(2,1)} custom-call(bf16[8,4,192,768]{3,2,1,0:T(8,128)(2,1)} %bitcast.43, f32[4,1,720]{2,1,0:T(1,128)} %reshape.82.gain, bf16[4,720,768]{2,1,0:T(8,128)(2,1)} %reshape_squeeze.12.weight_gu, bf16[4,720,128]{2,1,0:T(8,128)(2,1)} %bitcast.49, bf16[128,768]{1,0:T(8,128)(2,1)} %bitcast.48, ...), custom_call_target="tpu_custom_call" | custom-call | tf_op jit(solution)/shard_map/pallas_call | solution.py:347
  133.0 62.0 %shard_map.142 = bf16[192,720]{1,0:T(8,128)(2,1)} custom-call(bf16[4,2,2,2,192,720]{5,4,3,2,1,0:T(8,128)(2,1)} %bitcast.44), custom_call_target="tpu_custom_call" | custom-call | tf_op jit(solution)/shard_map/pallas_call | solution.py:277
  195.0 1.7 copy.38
  (7 shorter events, 0.0 us)
Async XLA Ops:
  7.2 9.9 %copy-start = (bf16[512,2880]{0,1:T(8,128)(2,1)S(1)}, bf16[512,2880]{0,1:T(8,128)(2,1)}, u32[]{:S(2)}) copy-start(bf16[512,2880]{0,1:T(8,128)(2,1)} %param.17) | copy-start | bytes 8847364
  7.2 44.0 %reduce-scatter.4.cloned.1.call-start = ((), (), s32[]{:S(2)}) async-start(), calls=%async_computation.1 | async-start | bytes 1843200
  8.4 6.8 %collective-permute-start = (bf16[127,1,128]{0,2,1:T(8,128)(2,1)S(1)}, bf16[127,1,128]{0,2,1:T(8,128)(2,1)S(1)}, u32[]{:S(2)}, u32[]{:S(2)}) collective-permute-start(bf16[127,1,128]{0,2,1:T(8,128)(2,1)S(1)} %slice.12), channel_id=1, source_target_pairs={{0,4},{4,8},{8,12},{12,16},{16,20},{20,24},{24,28},{1,5},{5,9},{9,... | collective-permute-start | bytes 97544 | tf_op jit(solution)/shard_map/ppermute | solution.py:18
  19.2 2.7 %copy-start.6 = (s32[192]{0:T(256)S(1)}, s32[192]{0:T(256)}, u32[]{:S(2)}) copy-start(s32[192]{0:T(256)} %param.21) | copy-start | bytes 2308
  19.2 2.8 %copy-start.4 = (s32[192,4]{0,1:T(4,128)S(1)}, s32[192,4]{0,1:T(4,128)}, u32[]{:S(2)}) copy-start(s32[192,4]{0,1:T(4,128)} %param.19) | copy-start | bytes 9220
  19.2 2.8 %copy-start.5 = (s32[192,4]{0,1:T(4,128)S(1)}, s32[192,4]{0,1:T(4,128)}, u32[]{:S(2)}) copy-start(s32[192,4]{0,1:T(4,128)} %param.20) | copy-start | bytes 9220
  19.2 2.8 %copy-start.3 = (f32[2880]{0:T(1024)S(1)}, f32[2880]{0:T(1024)}, u32[]{:S(2)}) copy-start(f32[2880]{0:T(1024)} %param.18) | copy-start | bytes 34564
  19.2 5.7 %copy-start.2 = (bf16[1,128,2,384]{3,2,1,0:T(2,128)(2,1)S(1)}, bf16[1,128,2,384]{3,2,1,0:T(2,128)(2,1)}, u32[]{:S(2)}) copy-start(bf16[1,128,2,384]{3,2,1,0:T(2,128)(2,1)} %param.24) | copy-start | bytes 589828
  53.3 55.5 %copy-start.1 = (bf16[192,720]{1,0:T(8,128)(2,1)}, bf16[192,720]{1,0:T(8,128)(2,1)S(1)}, u32[]{:S(2)}) copy-start(bf16[192,720]{1,0:T(8,128)(2,1)S(1)} %add_convert_fusion) | copy-start | bytes 829444
Sparse Core Ops, SparseCore 0:
  22.0 29.0 reduce-scatter.3

commit v3 on v2

--- a/solution.py
+++ b/solution.py
@@ -64,20 +64,19 @@
     )
     attended = attended.astype(jnp.bfloat16).reshape(tok_rows, heads_here * head_size)
     head_terms = jnp.dot(attended, out_proj, preferred_element_type=jnp.float32)
-    head_share = lax.psum_scatter(
-        head_terms.astype(jnp.bfloat16), "tp", scatter_dimension=1, tiled=True
-    ).astype(jnp.float32)
-    residual_out = (residual_in.astype(jnp.float32) + head_share).astype(jnp.bfloat16)
     sources = lax.axis_size("ex")
     experts_all = gate_up.shape[0] * sources
     capacity = 5 * tok_rows * TOP // (3 * experts_all)
     grouped = lax.axis_size("tp") == 4 and sources % 2 == 0
     if grouped and gate_up.shape[0] == 1 and 2 * capacity >= tok_rows and experts_all <= 256:
-        mixed = dense_experts(
-            residual_out, routes, route_scores, tenants,
+        return dense_experts(
+            head_terms, residual_in, routes, route_scores, tenants,
             norm_gain, gate_up, adapter_in, adapter_out, down_proj,
         )
-        return (residual_out, mixed)
+    head_share = lax.psum_scatter(
+        head_terms.astype(jnp.bfloat16), "tp", scatter_dimension=1, tiled=True
+    ).astype(jnp.float32)
+    residual_out = (residual_in.astype(jnp.float32) + head_share).astype(jnp.bfloat16)
     return (
         residual_out,
         routed_experts(
@@ -107,7 +106,7 @@
 
 
 def gather_kernel(
-    deep, mine, out, own_sem, z_send, z_recv, x_send, x_recv, y_send, y_recv,
+    deep, heads, base, out, block, mine, core_in, part, x_in, own_sem, h_send, h_recv, z_send, z_recv, x_send, x_recv, y_send, y_recv,
     dx_send, dx_recv, dy_send, dy_recv, c_send, c_recv,
 ):
     z, y, x, c = place()
@@ -129,11 +128,27 @@
     def whole(k, yy, xx, cc):
         return out.at[lax.rem(z - k + deep, deep), yy, xx, cc]
 
+    h_sems = (h_send, h_recv)
+    across = send(heads.at[1 - x, 1 - c], core_in.at[0], h_sems, 0, at_c)
+    here = send(heads.at[x, 1 - c], core_in.at[1], h_sems, 1, at_c)
+    across.wait_recv()
+    part[...] = (
+        heads[1 - x, c].astype(jnp.float32) + core_in[0].astype(jnp.float32)
+    ).astype(part.dtype)
+    over = send(part, x_in, h_sems, 2, at_x)
+    here.wait_recv()
+    total = base[...].astype(jnp.float32) + (
+        heads[x, c].astype(jnp.float32) + core_in[1].astype(jnp.float32)
+    )
+    over.wait_recv()
+    total = (total + x_in[...].astype(jnp.float32)).astype(mine.dtype)
+    mine[...] = total
+    block[...] = total
     own = pltpu.make_async_copy(mine, whole(0, y, x, c), own_sem)
     own.start()
     z_sems, x_sems, y_sems = (z_send, z_recv), (x_send, x_recv), (y_send, y_recv)
     dx_sems, dy_sems, c_sems = (dx_send, dx_recv), (dy_send, dy_recv), (c_send, c_recv)
-    sent = []
+    sent = [across, here, over]
     down = [None]
     for k in range(1, deep):
         copy = send(mine, whole(0, y, x, c), z_sems, k, device(lax.rem(z + k, deep), y, x, c))
@@ -171,17 +186,24 @@
         copy.wait_send()
 
 
-def gather_rows(block):
+def gather_rows(heads, base):
     deep = lax.axis_size("ex") // 2
     dma = pltpu.SemaphoreType.DMA
+    tile = pltpu.VMEM(base.shape, base.dtype)
     return pl.pallas_call(
         functools.partial(gather_kernel, deep),
-        out_shape=jax.ShapeDtypeStruct((deep, 2, 2, 2) + block.shape, block.dtype),
-        in_specs=[pl.BlockSpec(memory_space=pltpu.VMEM)],
-        out_specs=pl.BlockSpec(memory_space=pl.ANY),
-        scratch_shapes=[dma] + [dma((deep,))] * 10 + [dma((5 * deep,))] * 2,
+        out_shape=(
+            jax.ShapeDtypeStruct((deep, 2, 2, 2) + base.shape, base.dtype),
+            jax.ShapeDtypeStruct(base.shape, base.dtype),
+        ),
+        in_specs=[pl.BlockSpec(memory_space=pltpu.VMEM)] * 2,
+        out_specs=(pl.BlockSpec(memory_space=pl.ANY), pl.BlockSpec(memory_space=pltpu.VMEM)),
+        scratch_shapes=[tile, pltpu.VMEM((2,) + base.shape, base.dtype), tile, tile]
+        + [dma, dma((3,)), dma((3,))]
+        + [dma((deep,))] * 10
+        + [dma((5 * deep,))] * 2,
         compiler_params=pltpu.CompilerParams(collective_id=0, has_side_effects=True),
-    )(block)
+    )(heads.reshape((2, 2) + base.shape), base)
 
 
 def scatter_kernel(
@@ -330,18 +352,22 @@
 
 
 def dense_experts(
-    residual_out, routes, route_scores, tenants,
+    head_terms, residual_in, routes, route_scores, tenants,
     norm_gain, gate_up, adapter_in, adapter_out, down_proj,
 ):
-    tok_rows, columns = residual_out.shape
+    tok_rows, columns = residual_in.shape
     sources, quarters = lax.axis_size("ex"), lax.axis_size("tp")
     hidden = gate_up.shape[3]
     rank_cols = adapter_in.shape[2]
     meta = jnp.concatenate([routes, route_scores, tenants[:, None]], axis=1).astype(jnp.bfloat16)
     padded = -(-(columns + meta.shape[1]) // 128) * 128
     fill = jnp.zeros((tok_rows, padded - columns - meta.shape[1]), jnp.bfloat16)
-    block = jnp.concatenate([residual_out, meta, fill], axis=1)
-    tokens = gather_rows(block).reshape(sources, quarters, tok_rows, padded)
+    base = jnp.concatenate([residual_in, meta, fill], axis=1)
+    heads = head_terms.astype(jnp.bfloat16)
+    heads = [heads[:, q * columns : (q + 1) * columns] for q in range(quarters)]
+    heads = jnp.stack([jnp.pad(part, ((0, 0), (0, padded - columns))) for part in heads])
+    tokens, block = gather_rows(heads, base)
+    tokens = tokens.reshape(sources, quarters, tok_rows, padded)
     step = 2
     fixed = lambda *shape: pl.BlockSpec(shape, lambda i: (0,) * len(shape))
     terms = pl.pallas_call(
@@ -366,7 +392,7 @@
         adapter_out[0].reshape(rank_cols, 2 * hidden),
         down_proj[0].reshape(hidden, quarters, columns).transpose(1, 0, 2),
     )
-    return scatter_terms(terms)
+    return (block[:, :columns], scatter_terms(terms))
 
 
 def routed_experts(

time: 204 us -> 196 us (0.961)
  between operations: 14.2 us -> 0.77 us
  Pallas kernels: 140 us -> 152 us
  waiting for transfers between devices: 10.8 us -> 0.01 us
  other arithmetic: 1.28 us -> 4.17 us
    pallas_call x1, Pallas kernels: 53.7 us -> 64.7 us  [gather_rows(): pl.pallas_call(functools.partial(gather_kernel, deep), out_shape=(jax.Sha...]
    unnamed x2 -> x0, waiting for transfers between devices: 10.8 us -> none
    another operation x3 -> x5, other arithmetic: 0.01 us -> 3.31 us
    unnamed x20 -> x21, local copies, waits for them, and re-layouts: 8.36 us -> 6.18 us
  transfers between devices with their start and end apart: 2 -> 1, of which waited for: 1 -> 0; matrix products, arithmetic and copies ran while one was open for 10% -> 14% of each run, Pallas kernels for 0% -> 0%
where the time goes in v3:
time: 196 us
  Pallas kernels  152 us (78%)
  local copies, waits for them, and re-layouts  28.8 us (15%)
  starting transfers between devices  5.49 us (3%)
  matrix products  4.52 us (2%)
  other arithmetic  4.17 us (2%)
    pallas_call x1, Pallas kernels, gather_rows(): pl.pallas_call(functools.partial(gather_kernel, deep), out_shape=(jax.Sha...  64.7 us
    pallas_call x1, Pallas kernels, scatter_terms(): pl.pallas_call(functools.partial(scatter_kernel, deep), out_shape=jax.Sha...  63 us
    pallas_call x1, Pallas kernels, dense_experts(): pl.pallas_call(expert_kernel, grid=(sources // step,), out_shape=jax.Shap...  24.1 us
    another operation x1, local copies, waits for them, and re-layouts, dense_experts(): gate_up[0].reshape(quarters, columns, 2 * hidden)  10.6 us
    unnamed x21, local copies, waits for them, and re-layouts  6.18 us
    ppermute x1, starting transfers between devices, from_behind(): lax.ppermute(value, axis, [(source, source + steps) for source in range(i...  5.49 us
    another operation x1, local copies, waits for them, and re-layouts, dense_experts(): down_proj[0].reshape(hidden, quarters, columns).transpose(1, 0, 2)  4.24 us
  transfers between devices with their start and end apart: 1, of which 0 were waited for; matrix products, arithmetic and copies ran while one was open for 14% of the time, Pallas kernels for 0%

profile of v3, /device:TPU:0, one launch (start us, length us, event | category | flops | bytes accessed | tf_op | source)
XLA Modules:
  0.0 195.6 jit_solution(8868763934881137923)
XLA Ops:
  0.6 0.0 copy-start
  0.6 1.0 copy.20
  1.7 0.0 copy-start.3
  1.7 0.7 slice.33
  2.4 5.5 %collective-permute-start = (bf16[127,1,128]{0,2,1:T(8,128)(2,1)}, bf16[127,1,128]{0,2,1:T(8,128)(2,1)}, u32[]{:S(2)}, u32[]{:S(2)}) collective-permute-start(bf16[127,1,128]{0,2,1:T(8,128)(2,1)} %slice.33), channel_id=1, source_target_pairs={{0,4},{4,8},{8,12},{12,16},{16,20},{20,24},{24,28},{1,5},{5,9},{9,... | collective-permute-start | bytes 97544 | tf_op jit(solution)/shard_map/ppermute | solution.py:18
  7.9 0.8 fusion.4
  8.7 1.2 exp.16
  9.9 0.7 convert.12
  10.6 0.7 convert.10
  11.3 0.7 convert.11
  12.0 0.0 copy-done.3
  12.0 1.4 reshape.86.gain
  13.4 0.1 copy.24
  13.5 0.8 copy.23
  14.3 0.7 broadcast_in_dim.24
  15.0 1.6 copy.27
  16.6 1.1 copy.22
  17.7 4.2 %copy.26 = bf16[384,4,720]{2,0,1:T(8,128)(2,1)} copy(bf16[384,4,720]{0,2,1:T(8,128)(2,1)} %bitcast.55) | data formatting | bytes 4423680 | tf_op jit(solution)/shard_map/reshape;squeeze | solution.py:393
  21.9 0.0 copy-start.1
  21.9 10.6 %reshape_squeeze.12.weight_gu = bf16[4,720,768]{2,1,0:T(8,128)(2,1)} reshape(bf16[1,2880,2,384]{3,2,1,0:T(2,128)(2,1)} %param.22) | data formatting | bytes 8847360 | tf_op jit(solution)/shard_map/reshape;squeeze | solution.py:390
  32.6 0.6 broadcast_in_dim.23
  33.2 0.0 copy-done.1
  33.2 1.7 concatenate.10.base
  34.9 0.0 copy-start.7
  34.9 0.0 copy-start.4
  34.9 0.0 copy-start.5
  34.9 0.0 collective-permute-done
  34.9 1.9 fusion
  36.8 0.0 copy-done.7
  36.8 0.1 broadcast_add_fusion
  36.9 0.0 copy-done.4
  36.9 0.0 copy-done.5
  36.9 1.5 convolution_convert_fusion.1
  38.4 0.0 copy-done
  38.4 0.0 copy-start.6
  38.4 1.1 convolution_convert_fusion
  39.5 0.4 fusion.16
  40.0 0.0 copy-done.6
  40.0 0.1 fusion.2
  40.1 0.1 pad_bitcast_fusion
  40.1 1.2 pad_maximum_fusion
  41.3 64.7 %shard_map.140 = (bf16[4,2,2,2,192,768]{5,4,3,2,1,0:T(8,128)(2,1)}, bf16[192,768]{1,0:T(8,128)(2,1)}) custom-call(bf16[2,2,192,768]{3,2,1,0:T(8,128)(2,1)} %bitcast.54, bf16[192,768]{1,0:T(8,128)(2,1)} %concatenate.10.base), custom_call_target="tpu_custom_call" | custom-call | tf_op jit(solution)/shard_map/pallas_call | solution.py:193
  106.0 24.1 %shard_map.141 = bf16[8,4,192,720]{3,2,1,0:T(8,128)(2,1)} custom-call(bf16[8,4,192,768]{3,2,1,0:T(8,128)(2,1)} %bitcast.53, f32[4,1,720]{2,1,0:T(1,128)} %reshape.86.gain, bf16[4,720,768]{2,1,0:T(8,128)(2,1)} %reshape_squeeze.12.weight_gu, bf16[4,720,128]{2,1,0:T(8,128)(2,1)} %bitcast.57, bf16[128,768]{1,0:T(8,128)(2,1)} %bitcast.56, ...), custom_call_target="tpu_custom_call" | custom-call | tf_op jit(solution)/shard_map/pallas_call | solution.py:373
  130.2 0.0 copy-start.2
  130.2 63.0 %shard_map.142 = bf16[192,720]{1,0:T(8,128)(2,1)} custom-call(bf16[4,2,2,2,192,720]{5,4,3,2,1,0:T(8,128)(2,1)} %bitcast.51), custom_call_target="tpu_custom_call" | custom-call | tf_op jit(solution)/shard_map/pallas_call | solution.py:299
  193.2 0.0 copy-done.2
  193.2 0.7 copy.30
  193.9 1.7 copy.31
  (3 shorter events, 0.0 us)
Async XLA Ops:
  0.6 37.8 %copy-start = (bf16[512,2880]{0,1:T(8,128)(2,1)S(1)}, bf16[512,2880]{0,1:T(8,128)(2,1)}, u32[]{:S(2)}) copy-start(bf16[512,2880]{0,1:T(8,128)(2,1)} %param.17) | copy-start | bytes 8847364
  1.7 10.3 %copy-start.3 = (bf16[192,1,128]{0,2,1:T(8,128)(2,1)}, bf16[192,1,128]{0,2,1:T(8,128)(2,1)S(1)}, u32[]{:S(2)}) copy-start(bf16[192,1,128]{0,2,1:T(8,128)(2,1)S(1)} %copy.20) | copy-start | bytes 147460
  2.4 32.5 %collective-permute-start = (bf16[127,1,128]{0,2,1:T(8,128)(2,1)}, bf16[127,1,128]{0,2,1:T(8,128)(2,1)}, u32[]{:S(2)}, u32[]{:S(2)}) collective-permute-start(bf16[127,1,128]{0,2,1:T(8,128)(2,1)} %slice.33), channel_id=1, source_target_pairs={{0,4},{4,8},{8,12},{12,16},{16,20},{20,24},{24,28},{1,5},{5,9},{9,... | collective-permute-start | bytes 97544 | tf_op jit(solution)/shard_map/ppermute | solution.py:18
  21.9 11.3 %copy-start.1 = (bf16[192,720]{1,0:T(8,128)(2,1)S(1)}, bf16[192,720]{1,0:T(8,128)(2,1)}, u32[]{:S(2)}) copy-start(bf16[192,720]{1,0:T(8,128)(2,1)} %param.13) | copy-start | bytes 829444
  34.9 1.9 copy-start.7
  34.9 2.0 %copy-start.4 = (bf16[192,1,128]{0,2,1:T(8,128)(2,1)S(1)}, bf16[192,1,128]{0,2,1:T(8,128)(2,1)}, u32[]{:S(2)}) copy-start(bf16[192,1,128]{0,2,1:T(8,128)(2,1)} %copy-done.3) | copy-start | bytes 147460
  34.9 2.0 %copy-start.5 = (pred[192,319]{1,0:T(8,128)(4,1)S(1)}, pred[192,319]{1,0:T(8,128)(4,1)}, u32[]{:S(2)}) copy-start(pred[192,319]{1,0:T(8,128)(4,1)} %fusion.4) | copy-start | bytes 183748
  38.4 1.6 copy-start.6
  130.2 63.0 %copy-start.2 = (bf16[192,768]{1,0:T(8,128)(2,1)S(1)}, bf16[192,768]{1,0:T(8,128)(2,1)}, u32[]{:S(2)}) copy-start(bf16[192,768]{1,0:T(8,128)(2,1)} %get-tuple-element.4) | copy-start | bytes 884740

commit v4 on v3

--- a/solution.py
+++ b/solution.py
@@ -318,7 +318,7 @@
     held, quarters, tok_rows, padded = tokens.shape
     columns = gain.shape[2]
     rows = held * tok_rows
-    hidden = weight_down.shape[1]
+    hidden = weight_down.shape[2]
     rank_cols = weight_in.shape[2]
 
     def quarter(q):
@@ -347,7 +347,9 @@
     activated = gate_part * jax.nn.sigmoid(1.702 * gate_part) * (up_part + 1.0)
     activated = (activated * weight).astype(jnp.bfloat16)
     for q in range(quarters):
-        term = jnp.dot(activated, weight_down[q], preferred_element_type=jnp.float32)
+        term = lax.dot_general(
+            activated, weight_down[q], (((1,), (1,)), ((), ())), preferred_element_type=jnp.float32
+        )
         terms[:, q] = term.astype(jnp.bfloat16).reshape(held, tok_rows, columns)
 
 
@@ -380,17 +382,19 @@
             fixed(quarters, columns, 2 * hidden),
             fixed(quarters, columns, rank_cols),
             fixed(rank_cols, 2 * hidden),
-            fixed(quarters, hidden, columns),
+            fixed(quarters, columns, hidden),
         ],
         out_specs=pl.BlockSpec((step, quarters, tok_rows, columns), lambda i: (i, 0, 0, 0)),
         compiler_params=pltpu.CompilerParams(vmem_limit_bytes=60 * 1024 * 1024),
     )(
         tokens,
         norm_gain.reshape(quarters, 1, columns),
-        gate_up[0].reshape(quarters, columns, 2 * hidden),
+        jnp.concatenate([gate_up[0, :, 0], gate_up[0, :, 1]], axis=1).reshape(
+            quarters, columns, 2 * hidden
+        ),
         adapter_in[0].reshape(quarters, columns, rank_cols),
         adapter_out[0].reshape(rank_cols, 2 * hidden),
-        down_proj[0].reshape(hidden, quarters, columns).transpose(1, 0, 2),
+        down_proj[0].T.reshape(quarters, columns, hidden),
     )
     return (block[:, :columns], scatter_terms(terms))
 

time: 196 us -> 190 us (0.969)
  local copies, waits for them, and re-layouts: 28.8 us -> 22.2 us
    another operation x4 -> x2, local copies, waits for them, and re-layouts: 15.8 us -> 0.9 us  [the longest x1 10.6 us: dense_experts(): gate_up[0].reshape(quarters, columns, 2 * hidden)]
    slice x0 -> x1, local copies, waits for them, and re-layouts: none -> 9.74 us  [dense_experts(): gate_up[0, :, 0]]
    concatenate x0 -> x1, other arithmetic: none -> 2.42 us  [dense_experts(): jnp.concatenate([gate_up[0, :, 0], gate_up[0, :, 1]], axis=1)]
    another operation x3, other arithmetic: 2.06 us -> 0.01 us
    unnamed x21 -> x35, local copies, waits for them, and re-layouts: 6.18 us -> 6.03 us
  transfers between devices with their start and end apart: 1 -> 1, of which waited for: 0 -> 0; matrix products, arithmetic and copies ran while one was open for 14% -> 11% of each run, Pallas kernels for 0% -> 0%
where the time goes in v4:
time: 190 us; the launch traced here: 189 us
  Pallas kernels  152 us (80%)
  local copies, waits for them, and re-layouts  22.2 us (12%)
  starting transfers between devices  5.51 us (3%)
  other arithmetic  4.58 us (2%)
  matrix products  4.52 us (2%)
    pallas_call x1, Pallas kernels, gather_rows(): pl.pallas_call(functools.partial(gather_kernel, deep), out_shape=(jax.Sha...  64.7 us
    pallas_call x1, Pallas kernels, scatter_terms(): pl.pallas_call(functools.partial(scatter_kernel, deep), out_shape=jax.Sha...  63.1 us
    pallas_call x1, Pallas kernels, dense_experts(): pl.pallas_call(expert_kernel, grid=(sources // step,), out_shape=jax.Shap...  24.1 us
    slice x1, local copies, waits for them, and re-layouts, dense_experts(): gate_up[0, :, 0]  9.74 us
    unnamed x35, local copies, waits for them, and re-layouts  6.03 us
    ppermute x1, starting transfers between devices, from_behind(): lax.ppermute(value, axis, [(source, source + steps) for source in range(i...  5.51 us
  transfers between devices with their start and end apart: 1, of which 0 were waited for; matrix products, arithmetic and copies ran while one was open for 11% of the time, Pallas kernels for 0%

profile of v4, /device:TPU:0, one launch (start us, length us, event | category | flops | bytes accessed | tf_op | source)
XLA Modules:
  0.0 189.5 jit_solution(7116187322905283200)
XLA Ops:
  0.6 0.0 copy-start
  0.6 1.0 copy.20
  1.7 0.0 copy-start.4
  1.7 0.7 slice.41
  2.4 5.5 %collective-permute-start = (bf16[127,1,128]{0,2,1:T(8,128)(2,1)}, bf16[127,1,128]{0,2,1:T(8,128)(2,1)}, u32[]{:S(2)}, u32[]{:S(2)}) collective-permute-start(bf16[127,1,128]{0,2,1:T(8,128)(2,1)} %slice.41), channel_id=1, source_target_pairs={{0,4},{4,8},{8,12},{12,16},{16,20},{20,24},{24,28},{1,5},{5,9},{9,... | collective-permute-start | bytes 97544 | tf_op jit(solution)/shard_map/ppermute | solution.py:18
  7.9 9.7 %fusion.16 = (bf16[1,2880,1,384]{3,2,1,0:T(2,128)(2,1)S(1)}, bf16[1,2880,1,384]{3,2,1,0:T(2,128)(2,1)S(1)}) fusion(bf16[1,2880,2,384]{3,2,1,0:T(2,128)(2,1)} %param.22), kind=kLoop, calls=%fused_computation.33 | loop fusion | bytes 8847360 | tf_op jit(solution)/shard_map/slice | solution.py:392
  17.7 0.0 copy-done.4
  17.7 0.4 copy.28
  18.1 0.4 copy.29
  18.5 0.8 fusion.4
  19.3 0.0 copy-start.7
  19.3 0.0 copy-start.3
  19.3 0.0 copy-start.1
  19.3 2.4 %pad_maximum_fusion.weight_gu = bf16[4,720,768]{2,1,0:T(8,128)(2,1)} fusion(bf16[4,720,384]{2,1,0:T(8,128)(2,1)S(1)} %bitcast.59, bf16[4,720,384]{2,1,0:T(8,128)(2,1)S(1)} %bitcast.58), kind=kLoop, calls=%fused_computation | loop fusion | flops 8847360 | bytes 8847360 | tf_op jit(solution)/shard_map/concatenate | solution.py:392
  21.7 0.0 copy-done.13
  21.7 0.6 exp.16
  22.3 0.0 copy-done.12
  22.3 0.0 copy-done.8
  22.3 0.0 copy-done.9
  22.4 0.0 copy-done.7
  22.4 0.7 reshape.94.gain
  23.1 0.1 copy.24
  23.2 0.8 copy.23
  24.0 0.7 broadcast_in_dim.24
  24.7 0.0 copy-done.3
  24.7 0.7 copy.30
  25.4 1.1 copy.22
  26.4 0.6 broadcast_in_dim.23
  27.1 0.0 copy-done.1
  27.1 1.7 concatenate.18.base
  28.8 0.0 collective-permute-done
  28.8 1.9 fusion
  30.7 0.0 copy-done.11
  30.7 0.1 broadcast_add_fusion
  30.8 1.5 convolution_convert_fusion.1
  32.3 0.0 copy-done
  32.3 0.0 copy-start.10
  32.3 1.1 convolution_convert_fusion
  33.4 0.4 fusion.17
  33.8 0.0 copy-done.10
  33.8 0.1 fusion.2
  33.9 0.1 pad_bitcast_fusion
  34.0 1.2 pad_maximum_fusion.1
  35.2 64.7 %shard_map.140 = (bf16[4,2,2,2,192,768]{5,4,3,2,1,0:T(8,128)(2,1)}, bf16[192,768]{1,0:T(8,128)(2,1)}) custom-call(bf16[2,2,192,768]{3,2,1,0:T(8,128)(2,1)} %bitcast.60, bf16[192,768]{1,0:T(8,128)(2,1)} %concatenate.18.base), custom_call_target="tpu_custom_call" | custom-call | tf_op jit(solution)/shard_map/pallas_call | solution.py:193
  99.9 24.1 %shard_map.141 = bf16[8,4,192,720]{3,2,1,0:T(8,128)(2,1)} custom-call(bf16[8,4,192,768]{3,2,1,0:T(8,128)(2,1)} %bitcast.57, f32[4,1,720]{2,1,0:T(1,128)} %reshape.94.gain, bf16[4,720,768]{2,1,0:T(8,128)(2,1)} %pad_maximum_fusion.weight_gu, bf16[4,720,128]{2,1,0:T(8,128)(2,1)} %bitcast.63, bf16[128,768]{1,0:T(8,128)(2,1)} %bitcast.62, ...), custom_call_target="tpu_custom_call" | custom-call | tf_op jit(solution)/shard_map/pallas_call | solution.py:375
  123.9 63.1 %shard_map.142 = bf16[192,720]{1,0:T(8,128)(2,1)} custom-call(bf16[4,2,2,2,192,720]{5,4,3,2,1,0:T(8,128)(2,1)} %bitcast.56), custom_call_target="tpu_custom_call" | custom-call | tf_op jit(solution)/shard_map/pallas_call | solution.py:299
  187.0 0.7 copy.33
  187.8 1.7 copy.34
  (17 shorter events, 0.0 us)
Async XLA Ops:
  0.6 31.6 %copy-start = (bf16[512,2880]{0,1:T(8,128)(2,1)S(1)}, bf16[512,2880]{0,1:T(8,128)(2,1)}, u32[]{:S(2)}) copy-start(bf16[512,2880]{0,1:T(8,128)(2,1)} %param.17) | copy-start | bytes 8847364
  1.7 16.0 %copy-start.4 = (bf16[192,1,128]{0,2,1:T(8,128)(2,1)}, bf16[192,1,128]{0,2,1:T(8,128)(2,1)S(1)}, u32[]{:S(2)}) copy-start(bf16[192,1,128]{0,2,1:T(8,128)(2,1)S(1)} %copy.20) | copy-start | bytes 147460
  2.4 26.4 %collective-permute-start = (bf16[127,1,128]{0,2,1:T(8,128)(2,1)}, bf16[127,1,128]{0,2,1:T(8,128)(2,1)}, u32[]{:S(2)}, u32[]{:S(2)}) collective-permute-start(bf16[127,1,128]{0,2,1:T(8,128)(2,1)} %slice.41), channel_id=1, source_target_pairs={{0,4},{4,8},{8,12},{12,16},{16,20},{20,24},{24,28},{1,5},{5,9},{9,... | collective-permute-start | bytes 97544 | tf_op jit(solution)/shard_map/ppermute | solution.py:18
  19.2 2.5 %copy-start.13 = (f32[8]{0:T(128)S(1)}, f32[8]{0:T(128)}, u32[]{:S(2)}) copy-start(f32[8]{0:T(128)} %param.16) | copy-start | bytes 100
  19.3 3.1 %copy-start.12 = (s32[192]{0:T(256)S(1)}, s32[192]{0:T(256)}, u32[]{:S(2)}) copy-start(s32[192]{0:T(256)} %param.21) | copy-start | bytes 2308
  19.3 3.1 %copy-start.8 = (s32[192,4]{0,1:T(4,128)S(1)}, s32[192,4]{0,1:T(4,128)}, u32[]{:S(2)}) copy-start(s32[192,4]{0,1:T(4,128)} %param.19) | copy-start | bytes 9220
  19.3 3.1 %copy-start.9 = (s32[192,4]{0,1:T(4,128)S(1)}, s32[192,4]{0,1:T(4,128)}, u32[]{:S(2)}) copy-start(s32[192,4]{0,1:T(4,128)} %param.20) | copy-start | bytes 9220
  19.3 3.1 %copy-start.7 = (f32[2880]{0:T(1024)S(1)}, f32[2880]{0:T(1024)}, u32[]{:S(2)}) copy-start(f32[2880]{0:T(1024)} %param.18) | copy-start | bytes 34564
  19.3 5.4 %copy-start.3 = (bf16[1,128,2,384]{3,2,1,0:T(2,128)(2,1)S(1)}, bf16[1,128,2,384]{3,2,1,0:T(2,128)(2,1)}, u32[]{:S(2)}) copy-start(bf16[1,128,2,384]{3,2,1,0:T(2,128)(2,1)} %param.24) | copy-start | bytes 589828
  19.3 7.8 %copy-start.1 = (bf16[192,720]{1,0:T(8,128)(2,1)S(1)}, bf16[192,720]{1,0:T(8,128)(2,1)}, u32[]{:S(2)}) copy-start(bf16[192,720]{1,0:T(8,128)(2,1)} %param.13) | copy-start | bytes 829444
  28.8 1.9 %copy-start.11 = (f32[8]{0:T(128)S(1)}, f32[8]{0:T(128)}, u32[]{:S(2)}) copy-start(f32[8]{0:T(128)} %exp.16) | copy-start | bytes 100
  28.8 2.0 %copy-start.5 = (bf16[192,1,128]{0,2,1:T(8,128)(2,1)S(1)}, bf16[192,1,128]{0,2,1:T(8,128)(2,1)}, u32[]{:S(2)}) copy-start(bf16[192,1,128]{0,2,1:T(8,128)(2,1)} %copy-done.4) | copy-start | bytes 147460
  28.8 2.0 %copy-start.6 = (pred[192,319]{1,0:T(8,128)(4,1)S(1)}, pred[192,319]{1,0:T(8,128)(4,1)}, u32[]{:S(2)}) copy-start(pred[192,319]{1,0:T(8,128)(4,1)} %fusion.4) | copy-start | bytes 183748
  32.3 1.6 copy-start.10
  123.9 63.1 %copy-start.2 = (bf16[192,768]{1,0:T(8,128)(2,1)S(1)}, bf16[192,768]{1,0:T(8,128)(2,1)}, u32[]{:S(2)}) copy-start(bf16[192,768]{1,0:T(8,128)(2,1)} %get-tuple-element.4) | copy-start | bytes 884740
